TPU v7x, 32 devices: a whole 2x2x4 slice. The times are simulated.
32 devices in a mesh: seq: 8 (over z, y), pass: 4 (over x, core).
Axes of the slice: x: 2, y: 2, z: 4, core: 2. Of those that a mesh axis runs over, the one named last changes fastest.
Arguments:
- x_rows: bfloat16 [4, 8192, 768], P('pass', 'seq'), may hold values from -6 to 6
- pass_depth: int32 [8, 1024], P('seq'), may hold values from 1 to 4
- cotangent: bfloat16 [4, 8192, 768], P('pass', 'seq'), may hold values from -6 to 6
- pass_emb: float32 [4, 768], replicated, may hold values from -3 to 3
- ln1_gain: float32 [768], replicated, may hold values from 0.1 to 1.9
- ln1_bias: float32 [768], replicated, may hold values from -2 to 2
- w_qkv: bfloat16 [768, 2304], P(('seq', 'pass')), may hold values from -0.21875 to 0.21875
- q_bias: float32 [768], replicated, may hold values from -2 to 2
- v_bias: float32 [768], replicated, may hold values from -0.6 to 0.6
- w_out: bfloat16 [768, 768], P(('seq', 'pass')), may hold values from -0.875 to 0.875
- out_bias: float32 [768], replicated, may hold values from -2 to 2
- ln2_gain: float32 [768], replicated, may hold values from 0.1 to 1.9
- ln2_bias: float32 [768], replicated, may hold values from -2 to 2
- w_up: bfloat16 [768, 3072], P(('seq', 'pass')), may hold values from -0.21875 to 0.21875
- up_bias: float32 [3072], replicated, may hold values from -3 to 3
- w_down: bfloat16 [3072, 768], P(('seq', 'pass')), may hold values from -0.109375 to 0.109375
- down_bias: float32 [768], replicated, may hold values from -2 to 2
Outputs:
- out_rows: bfloat16 [4, 8192, 768], P('pass', 'seq')
- x_grad: float32 [4, 8192, 768], P('pass', 'seq')
- w_qkv_grad: float32 [768, 2304], P(('seq', 'pass'))
- q_bias_grad: float32 [768], replicated
- v_bias_grad: float32 [768], replicated
- w_out_grad: float32 [768, 768], P(('seq', 'pass'))
- out_bias_grad: float32 [768], replicated
- ln1_gain_grad: float32 [768], replicated
- ln1_bias_grad: float32 [768], replicated
- ln2_gain_grad: float32 [768], replicated
- ln2_bias_grad: float32 [768], replicated
- w_up_grad: float32 [768, 3072], P(('seq', 'pass'))
- up_bias_grad: float32 [3072], replicated
- w_down_grad: float32 [3072, 768], P(('seq', 'pass'))
- down_bias_grad: float32 [768], replicated
- pass_emb_grad: float32 [4, 768], P('pass')
Inputs may be any that keep to these rules, and one draw needn't show every extreme that they name: A token serves as a key in its first pass_depth passes only; every token counts as a key in pass 0.
All inputs are finite; a program needn't handle non-finite values.
Results may differ from a plain program's by a relative error of at most 0.012.
Values may be sent and summed in bfloat16 or wider, within the bound.
No kernel may reach another device: no remote copies, remote signals or barrier semaphores. Data moves between devices by JAX's collectives and lax.ppermute only.
A program may use at most 256 MiB of HBM per device.

v0:
```python
from functools import partial
import math

import jax
import jax.numpy as jnp
from jax import lax
from jax.sharding import PartitionSpec as P

HEADS = 12
HEAD_DIM = 64


norm_eps = 1e-05


def layer_norm(values, gain_row, shift_row):
    center = values - jnp.mean(values, axis=-1, keepdims=True)
    inverse = lax.rsqrt(jnp.mean(center * center, axis=-1, keepdims=True) + norm_eps)
    return center * inverse * gain_row + shift_row


def gelu_exact(values):
    return jax.nn.gelu(values, approximate=False)


def matmul(first_op, second_op):
    return jnp.dot(first_op, second_op, preferred_element_type=jnp.float32)


def matmul_tn(first_op, second_op):
    return lax.dot_general(
        first_op, second_op, (((0,), (0,)), ((), ())), preferred_element_type=jnp.float32
    )


def matmul_nt(first_op, second_op):
    return lax.dot_general(
        first_op, second_op, (((1,), (1,)), ((), ())), preferred_element_type=jnp.float32
    )


def per_device(
    x_rows,
    pass_depth,
    cotangent,
    pass_emb,
    ln1_gain,
    ln1_bias,
    w_qkv,
    q_bias,
    v_bias,
    w_out,
    out_bias,
    ln2_gain,
    ln2_bias,
    w_up,
    up_bias,
    w_down,
    down_bias,
):
    bfloat = jnp.bfloat16
    model_width = x_rows.shape[2]
    seq_count, seq_len = pass_depth.shape
    passes = lax.axis_size("pass")
    pass_id = lax.axis_index("pass")
    key_total = passes * seq_len
    block_rows = math.gcd(seq_len, 512)
    block_count = seq_len // block_rows
    score_scale = HEAD_DIM ** (-0.5)

    def split_heads(flat_rows, lead_count):
        shaped = flat_rows.reshape(lead_count, seq_count, seq_len, HEADS, HEAD_DIM)
        return shaped.transpose(1, 3, 0, 2, 4).reshape(
            seq_count, HEADS, lead_count * seq_len, HEAD_DIM
        )

    def merge_heads(split_rows, lead_count):
        shaped = split_rows.reshape(seq_count, HEADS, lead_count, seq_len, HEAD_DIM)
        return shaped.transpose(2, 0, 3, 1, 4).reshape(
            lead_count * seq_count * seq_len, HEADS * HEAD_DIM
        )

    full_qkv, full_out, full_up, full_down = (
        lax.all_gather(w_qkv, ("seq", "pass"), axis=0, tiled=True),
        lax.all_gather(w_out, ("seq", "pass"), axis=0, tiled=True),
        lax.all_gather(w_up, ("seq", "pass"), axis=0, tiled=True),
        lax.all_gather(w_down, ("seq", "pass"), axis=0, tiled=True),
    )
    pass_row = lax.dynamic_index_in_dim(pass_emb, pass_id, 0, keepdims=False)
    stream_in = x_rows[0].astype(jnp.float32) + pass_row
    normed_one, norm_one_back = jax.vjp(layer_norm, stream_in, ln1_gain, ln1_bias)
    normed_one = normed_one.astype(bfloat)
    projected = matmul(normed_one, full_qkv)
    queries = (projected[:, :model_width] + q_bias).astype(bfloat)
    key_rows = projected[:, model_width : 2 * model_width].astype(bfloat)
    value_rows = (projected[:, 2 * model_width :] + v_bias).astype(bfloat)
    all_keys, all_values = (
        lax.all_gather(key_rows, "pass", axis=0, tiled=True),
        lax.all_gather(value_rows, "pass", axis=0, tiled=True),
    )
    query_heads = split_heads(queries, 1)
    key_heads = split_heads(all_keys, passes)
    value_heads = split_heads(all_values, passes)
    item_index = jnp.arange(seq_count * HEADS, dtype=jnp.int32)
    item_list = (item_index // HEADS, item_index % HEADS)

    def item_slices(item, kept):
        seq_index, head_index = item
        query_all = lax.dynamic_slice(
            query_heads, (seq_index, head_index, 0, 0), (1, 1, seq_len, HEAD_DIM)
        )[0, 0]
        key_all = lax.dynamic_slice(
            key_heads, (seq_index, head_index, 0, 0), (1, 1, key_total, HEAD_DIM)
        )[0, 0]
        value_all = lax.dynamic_slice(
            value_heads, (seq_index, head_index, 0, 0), (1, 1, key_total, HEAD_DIM)
        )[0, 0]
        key_all = key_all.reshape(passes, seq_len, HEAD_DIM)[:kept]
        value_all = value_all.reshape(passes, seq_len, HEAD_DIM)[:kept]
        depth_row = lax.dynamic_index_in_dim(pass_depth, seq_index, 0, keepdims=False)
        return (query_all, key_all, value_all, depth_row)

    def block_scores(kept, query_all, key_all, value_all, depth_row, block_index):
        end_row = (block_index + 1) * block_rows
        key_part = key_all[:, :end_row].reshape(kept * end_row, HEAD_DIM)
        value_part = value_all[:, :end_row].reshape(kept * end_row, HEAD_DIM)
        key_pass = jnp.repeat(jnp.arange(kept, dtype=jnp.int32), end_row)
        key_pos = jnp.tile(jnp.arange(end_row, dtype=jnp.int32), kept)
        key_valid = key_pass < jnp.tile(depth_row[:end_row], kept)
        query_part = query_all[block_index * block_rows : end_row]
        query_pos = block_index * block_rows + jnp.arange(block_rows, dtype=jnp.int32)
        allowed = key_valid[None, :] & (key_pos[None, :] <= query_pos[:, None])
        raw_scores = matmul_nt(query_part, key_part) * score_scale
        return (query_part, key_part, value_part, jnp.where(allowed, raw_scores, -1e30))

    def attend_kept(kept, item):
        query_all, key_all, value_all, depth_row = item_slices(item, kept)
        outputs = []
        sums = []
        for block_index in range(block_count):
            query_part, key_part, value_part, scores = block_scores(
                kept, query_all, key_all, value_all, depth_row, block_index
            )
            row_max = jnp.max(scores, axis=-1, keepdims=True)
            exp_scores = jnp.exp(scores - row_max)
            row_sum = jnp.sum(exp_scores, axis=-1, keepdims=True)
            prob_low = (exp_scores / row_sum).astype(bfloat)
            outputs.append(matmul(prob_low, value_part).astype(bfloat))
            sums.append(row_max[:, 0] + jnp.log(row_sum[:, 0]))
        return (jnp.concatenate(outputs, axis=0), jnp.concatenate(sums, axis=0))

    def attend(item):
        return lax.switch(
            pass_id, [partial(attend_kept, kept) for kept in range(1, passes + 1)], item
        )

    head_out, log_sums = lax.map(attend, item_list)
    attn_rows = merge_heads(head_out.reshape(seq_count, HEADS, seq_len, HEAD_DIM), 1)
    mixed = stream_in + matmul(attn_rows, full_out) + out_bias
    normed_two, norm_two_back = jax.vjp(layer_norm, mixed, ln2_gain, ln2_bias)
    normed_two = normed_two.astype(bfloat)
    upper = matmul(normed_two, full_up) + up_bias
    activated, gelu_back = jax.vjp(gelu_exact, upper)
    activated = activated.astype(bfloat)
    out_rows = (mixed + matmul(activated, full_down) + down_bias).astype(bfloat)
    full_qkv, full_out, full_up, full_down = (
        lax.all_gather(w_qkv, ("seq", "pass"), axis=0, tiled=True),
        lax.all_gather(w_out, ("seq", "pass"), axis=0, tiled=True),
        lax.all_gather(w_up, ("seq", "pass"), axis=0, tiled=True),
        lax.all_gather(w_down, ("seq", "pass"), axis=0, tiled=True),
    )
    out_grad = cotangent[0].astype(jnp.float32)
    down_low = out_grad.astype(bfloat)
    down_grad = matmul_tn(activated, down_low)
    (upper_grad,) = gelu_back(matmul_nt(down_low, full_down))
    upper_low = upper_grad.astype(bfloat)
    up_grad = matmul_tn(normed_two, upper_low)
    mixed_part, ln2_gain_part, ln2_bias_part = norm_two_back(matmul_nt(upper_low, full_up))
    mixed_grad = out_grad + mixed_part
    proj_low = mixed_grad.astype(bfloat)
    out_weight_grad = matmul_tn(attn_rows, proj_low)
    attn_grad = matmul_nt(proj_low, full_out).astype(bfloat)
    grad_heads = split_heads(attn_grad, 1)

    def attend_back_kept(kept, item_and_sum):
        item, log_sum = item_and_sum
        seq_index, head_index = item
        query_all, key_all, value_all, depth_row = item_slices(item, kept)
        grad_all = lax.dynamic_slice(
            grad_heads, (seq_index, head_index, 0, 0), (1, 1, seq_len, HEAD_DIM)
        )[0, 0]
        key_acc = jnp.zeros((kept, seq_len, HEAD_DIM), jnp.float32)
        value_acc = jnp.zeros((kept, seq_len, HEAD_DIM), jnp.float32)
        query_pieces = []
        for block_index in range(block_count):
            end_row = (block_index + 1) * block_rows
            query_part, key_part, value_part, scores = block_scores(
                kept, query_all, key_all, value_all, depth_row, block_index
            )
            attn_prob = jnp.exp(scores - log_sum[block_index * block_rows : end_row, None])
            grad_part = grad_all[block_index * block_rows : end_row]
            prob_grad = matmul_nt(grad_part, value_part)
            score_grad = (
                attn_prob * (prob_grad - jnp.sum(attn_prob * prob_grad, axis=-1, keepdims=True))
            ).astype(bfloat)
            query_pieces.append(matmul(score_grad, key_part) * score_scale)
            key_term = matmul_tn(score_grad, query_part) * score_scale
            value_term = matmul_tn(attn_prob.astype(bfloat), grad_part)
            key_acc = key_acc.at[:, :end_row].add(key_term.reshape(kept, end_row, HEAD_DIM))
            value_acc = value_acc.at[:, :end_row].add(value_term.reshape(kept, end_row, HEAD_DIM))
        key_full = jnp.zeros((passes, seq_len, HEAD_DIM), jnp.float32).at[:kept].set(key_acc)
        value_full = jnp.zeros((passes, seq_len, HEAD_DIM), jnp.float32).at[:kept].set(value_acc)
        return (
            jnp.concatenate(query_pieces, axis=0),
            key_full.reshape(key_total, HEAD_DIM),
            value_full.reshape(key_total, HEAD_DIM),
        )

    def attend_back(item_and_sum):
        return lax.switch(
            pass_id,
            [partial(attend_back_kept, kept) for kept in range(1, passes + 1)],
            item_and_sum,
        )

    query_grads, key_grads, value_grads = lax.map(attend_back, (item_list, log_sums))

    def whole_rows(per_item):
        return merge_heads(per_item.reshape(seq_count, HEADS, key_total, HEAD_DIM), passes)

    own_keys, own_values = (
        lax.psum_scatter(
            whole_rows(key_grads).astype(jnp.bfloat16), "pass", scatter_dimension=0, tiled=True
        ).astype(jnp.float32),
        lax.psum_scatter(
            whole_rows(value_grads).astype(jnp.bfloat16), "pass", scatter_dimension=0, tiled=True
        ).astype(jnp.float32),
    )
    query_low = merge_heads(query_grads.reshape(seq_count, HEADS, seq_len, HEAD_DIM), 1).astype(
        bfloat
    )
    key_low = own_keys.astype(bfloat)
    value_low = own_values.astype(bfloat)
    qkv_low = jnp.concatenate([query_low, key_low, value_low], axis=1)
    qkv_grad = matmul_tn(normed_one, qkv_low)
    stream_part, ln1_gain_part, ln1_bias_part = norm_one_back(matmul_nt(qkv_low, full_qkv))
    stream_grad = mixed_grad + stream_part
    pass_select = (jnp.arange(passes, dtype=jnp.int32) == pass_id).astype(jnp.float32)
    pass_part = pass_select[:, None] * jnp.sum(stream_grad, axis=0)[None, :]
    shard_qkv, shard_out, shard_up, shard_down = (
        lax.psum_scatter(qkv_grad, ("seq", "pass"), scatter_dimension=0, tiled=True),
        lax.psum_scatter(out_weight_grad, ("seq", "pass"), scatter_dimension=0, tiled=True),
        lax.psum_scatter(up_grad, ("seq", "pass"), scatter_dimension=0, tiled=True),
        lax.psum_scatter(down_grad, ("seq", "pass"), scatter_dimension=0, tiled=True),
    )
    (
        gain_one,
        shift_one,
        query_bias_sum,
        value_bias_sum,
        out_bias_sum,
        gain_two,
        shift_two,
        up_bias_sum,
        down_bias_sum,
        pass_total,
    ) = lax.psum(
        (
            ln1_gain_part,
            ln1_bias_part,
            jnp.sum(query_low.astype(jnp.float32), axis=0),
            jnp.sum(value_low.astype(jnp.float32), axis=0),
            jnp.sum(mixed_grad, axis=0),
            ln2_gain_part,
            ln2_bias_part,
            jnp.sum(upper_low.astype(jnp.float32), axis=0),
            jnp.sum(out_grad, axis=0),
            pass_part,
        ),
        ("seq", "pass"),
    )
    pass_grad = lax.dynamic_slice_in_dim(pass_total, pass_id, 1, 0)
    return (
        out_rows[None],
        stream_grad[None],
        shard_qkv,
        query_bias_sum,
        value_bias_sum,
        shard_out,
        out_bias_sum,
        gain_one,
        shift_one,
        gain_two,
        shift_two,
        shard_up,
        up_bias_sum,
        shard_down,
        down_bias_sum,
        pass_grad,
    )


def solution(mesh):
    placed = (
        P("pass", "seq", None),
        P("seq", None),
        P("pass", "seq", None),
        P(),
        P(),
        P(),
        P(("seq", "pass"), None),
        P(),
        P(),
        P(("seq", "pass"), None),
        P(),
        P(),
        P(),
        P(("seq", "pass"), None),
        P(),
        P(("seq", "pass"), None),
        P(),
    )
    return jax.shard_map(
        per_device,
        mesh=mesh,
        in_specs=placed,
        out_specs=(
            P("pass", "seq", None),
            P("pass", "seq", None),
            P(("seq", "pass"), None),
            P(),
            P(),
            P(("seq", "pass"), None),
            P(),
            P(),
            P(),
            P(),
            P(),
            P(("seq", "pass"), None),
            P(),
            P(("seq", "pass"), None),
            P(),
            P("pass", None),
        ),
        check_vma=False,
    )
```

profile of v0, /device:TPU:0, one launch (start us, length us, event | category | flops | bytes accessed | tf_op | source)
XLA Modules:
  0.0 2400.3 jit_solution(17493814154461534555)
XLA Ops:
  10.8 62.9 %all-gather.7.cloned.1.call-done = bf16[768,2304]{1,0:T(8,128)(2,1)} async-done(((bf16[24,2304]{1,0:T(8,128)(2,1)}), bf16[768,2304]{1,0:T(8,128)(2,1)}) %all-gather.7.cloned.1.call-update) | async-done | bytes 3538960 | tf_op jit(solution)/shard_map/all_gather | solution.py:84
  94.8 35.0 %all-gather.11.cloned.1.call-done = bf16[4096,768]{1,0:T(8,128)(2,1)} async-done(((bf16[1024,768]{1,0:T(8,128)(2,1)}), bf16[4096,768]{1,0:T(8,128)(2,1)}) %all-gather.11.cloned.1.call-update) | async-done | bytes 6291472 | tf_op jit(solution)/shard_map/all_gather | solution.py:99
  138.5 11.4 reshape.1447
  150.0 14.1 copy.91
  164.1 13.6 all-gather.9.cloned.1.call-done
  186.5 11.2 reshape.1445
  197.7 14.2 copy.90
  212.4 155.0 %while.64 = (s32[]{:T(128)}, bf16[12,1024,64]{1,2,0:T(8,128)(2,1)}, f32[12,1024]{1,0:T(8,128)}, s32[12]{0:T(128)}, s32[1,1024]{1,0:T(1,128)S(1)}, /*index=5*/bf1...) while((s32[]{:T(128)}, bf16[12,1024,64]{1,2,0:T(8,128)(2,1)}, ...), condition=%wide.region_23.24_spmd, body=%wide.region_2.23_spmd.sunk | while | flops 837097984 | bytes 77652256 | solution.py:157
  213.9 8.8 conditional.4
  226.0 8.8 conditional.4
  238.1 8.8 conditional.4
  262.4 8.8 conditional.4
  274.5 8.8 conditional.4
  286.6 8.8 conditional.4
  323.0 8.8 conditional.4
  335.1 8.8 conditional.4
  347.2 8.8 conditional.4
  372.2 38.4 %multiply_convert_fusion.8 = (bf16[1024,3072]{1,0:T(8,128)(2,1)}, f32[1024,3072]{1,0:T(8,128)}, f32[1024,3072]{1,0:T(8,128)}) fusion(f32[3072]{0:T(1024)S(1)} %copy-done.58, bf16[768,3072]{1,0:T(8,128)(2,1)} %all-gather.15.cloned.1.call-done, f32[1024,768]{0,1:T(8,128)S(1)} %get-tuple-element.1126, f32[768]{0:T(1024)S(1)} %copy-done.59, ...), kind=kOutput, calls=%fused_computation.371 | convolution fusion | flops 5043388416 | bytes 39348224 | tf_op jit(solution)/shard_map/dot_general | solution.py:27
  410.6 19.0 convert_reduce_fusion
  429.6 10.3 fusion.231
  453.3 448.2 %while.65 = (s32[]{:T(128)}, bf16[12,1024,64]{1,2,0:T(8,128)(2,1)}, bf16[12,4096,64]{1,2,0:T(8,128)(2,1)}, bf16[12,4096,64]{1,2,0:T(8,128)(2,1)}, s32[12]{0:T(12...) while((s32[]{:T(128)}, bf16[12,1024,64]{1,2,0:T(8,128)(2,1)}, ...), condition=%wide.region_41.42_spmd, body=%wide.region_28.41_spmd.sunk | while | flops 2081166848 | bytes 146125840 | solution.py:226
  455.5 43.3 %conditional.5 = (bf16[1,1024,64]{1,2,0:T(8,128)(2,1)}, bf16[1,4096,64]{1,2,0:T(8,128)(2,1)}, bf16[1,4096,64]{1,2,0:T(8,128)(2,1)}) conditional(s32[]{:T(128)} %get-tuple-element.1366, (s32[1,1024]{1,0:T(1,128)S(1)}, s32[]{:T(128)}, bf16[1,12,1024,64]{3,2,1,0:T(8,128)(2,1)}, bf16[1,12,4096,64]{3,2,1,0:T(8,128)(2,1)}, ...), branch_computations={%region_29.31_spmd, %region_32.34_spmd, %region_35.37_spmd, %regio... | conditional | flops 2081166848 | bytes 143756960 | solution.py:220
  505.4 30.0 %conditional.5 = (bf16[1,1024,64]{1,2,0:T(8,128)(2,1)}, bf16[1,4096,64]{1,2,0:T(8,128)(2,1)}, bf16[1,4096,64]{1,2,0:T(8,128)(2,1)}) conditional(s32[]{:T(128)} %get-tuple-element.1366, (s32[1,1024]{1,0:T(1,128)S(1)}, s32[]{:T(128)}, bf16[1,12,1024,64]{3,2,1,0:T(8,128)(2,1)}, bf16[1,12,4096,64]{3,2,1,0:T(8,128)(2,1)}, ...), branch_computations={%region_29.31_spmd, %region_32.34_spmd, %region_35.37_spmd, %regio... | conditional | flops 2081166848 | bytes 143756960 | solution.py:220
  541.2 29.7 %conditional.5 = (bf16[1,1024,64]{1,2,0:T(8,128)(2,1)}, bf16[1,4096,64]{1,2,0:T(8,128)(2,1)}, bf16[1,4096,64]{1,2,0:T(8,128)(2,1)}) conditional(s32[]{:T(128)} %get-tuple-element.1366, (s32[1,1024]{1,0:T(1,128)S(1)}, s32[]{:T(128)}, bf16[1,12,1024,64]{3,2,1,0:T(8,128)(2,1)}, bf16[1,12,4096,64]{3,2,1,0:T(8,128)(2,1)}, ...), branch_computations={%region_29.31_spmd, %region_32.34_spmd, %region_35.37_spmd, %regio... | conditional | flops 2081166848 | bytes 143756960 | solution.py:220
  576.6 29.7 %conditional.5 = (bf16[1,1024,64]{1,2,0:T(8,128)(2,1)}, bf16[1,4096,64]{1,2,0:T(8,128)(2,1)}, bf16[1,4096,64]{1,2,0:T(8,128)(2,1)}) conditional(s32[]{:T(128)} %get-tuple-element.1366, (s32[1,1024]{1,0:T(1,128)S(1)}, s32[]{:T(128)}, bf16[1,12,1024,64]{3,2,1,0:T(8,128)(2,1)}, bf16[1,12,4096,64]{3,2,1,0:T(8,128)(2,1)}, ...), branch_computations={%region_29.31_spmd, %region_32.34_spmd, %region_35.37_spmd, %regio... | conditional | flops 2081166848 | bytes 143756960 | solution.py:220
  612.1 29.7 %conditional.5 = (bf16[1,1024,64]{1,2,0:T(8,128)(2,1)}, bf16[1,4096,64]{1,2,0:T(8,128)(2,1)}, bf16[1,4096,64]{1,2,0:T(8,128)(2,1)}) conditional(s32[]{:T(128)} %get-tuple-element.1366, (s32[1,1024]{1,0:T(1,128)S(1)}, s32[]{:T(128)}, bf16[1,12,1024,64]{3,2,1,0:T(8,128)(2,1)}, bf16[1,12,4096,64]{3,2,1,0:T(8,128)(2,1)}, ...), branch_computations={%region_29.31_spmd, %region_32.34_spmd, %region_35.37_spmd, %regio... | conditional | flops 2081166848 | bytes 143756960 | solution.py:220
  647.6 29.7 %conditional.5 = (bf16[1,1024,64]{1,2,0:T(8,128)(2,1)}, bf16[1,4096,64]{1,2,0:T(8,128)(2,1)}, bf16[1,4096,64]{1,2,0:T(8,128)(2,1)}) conditional(s32[]{:T(128)} %get-tuple-element.1366, (s32[1,1024]{1,0:T(1,128)S(1)}, s32[]{:T(128)}, bf16[1,12,1024,64]{3,2,1,0:T(8,128)(2,1)}, bf16[1,12,4096,64]{3,2,1,0:T(8,128)(2,1)}, ...), branch_computations={%region_29.31_spmd, %region_32.34_spmd, %region_35.37_spmd, %regio... | conditional | flops 2081166848 | bytes 143756960 | solution.py:220
  683.0 29.7 %conditional.5 = (bf16[1,1024,64]{1,2,0:T(8,128)(2,1)}, bf16[1,4096,64]{1,2,0:T(8,128)(2,1)}, bf16[1,4096,64]{1,2,0:T(8,128)(2,1)}) conditional(s32[]{:T(128)} %get-tuple-element.1366, (s32[1,1024]{1,0:T(1,128)S(1)}, s32[]{:T(128)}, bf16[1,12,1024,64]{3,2,1,0:T(8,128)(2,1)}, bf16[1,12,4096,64]{3,2,1,0:T(8,128)(2,1)}, ...), branch_computations={%region_29.31_spmd, %region_32.34_spmd, %region_35.37_spmd, %regio... | conditional | flops 2081166848 | bytes 143756960 | solution.py:220
  718.5 29.7 %conditional.5 = (bf16[1,1024,64]{1,2,0:T(8,128)(2,1)}, bf16[1,4096,64]{1,2,0:T(8,128)(2,1)}, bf16[1,4096,64]{1,2,0:T(8,128)(2,1)}) conditional(s32[]{:T(128)} %get-tuple-element.1366, (s32[1,1024]{1,0:T(1,128)S(1)}, s32[]{:T(128)}, bf16[1,12,1024,64]{3,2,1,0:T(8,128)(2,1)}, bf16[1,12,4096,64]{3,2,1,0:T(8,128)(2,1)}, ...), branch_computations={%region_29.31_spmd, %region_32.34_spmd, %region_35.37_spmd, %regio... | conditional | flops 2081166848 | bytes 143756960 | solution.py:220
  753.9 29.7 %conditional.5 = (bf16[1,1024,64]{1,2,0:T(8,128)(2,1)}, bf16[1,4096,64]{1,2,0:T(8,128)(2,1)}, bf16[1,4096,64]{1,2,0:T(8,128)(2,1)}) conditional(s32[]{:T(128)} %get-tuple-element.1366, (s32[1,1024]{1,0:T(1,128)S(1)}, s32[]{:T(128)}, bf16[1,12,1024,64]{3,2,1,0:T(8,128)(2,1)}, bf16[1,12,4096,64]{3,2,1,0:T(8,128)(2,1)}, ...), branch_computations={%region_29.31_spmd, %region_32.34_spmd, %region_35.37_spmd, %regio... | conditional | flops 2081166848 | bytes 143756960 | solution.py:220
  789.3 29.7 %conditional.5 = (bf16[1,1024,64]{1,2,0:T(8,128)(2,1)}, bf16[1,4096,64]{1,2,0:T(8,128)(2,1)}, bf16[1,4096,64]{1,2,0:T(8,128)(2,1)}) conditional(s32[]{:T(128)} %get-tuple-element.1366, (s32[1,1024]{1,0:T(1,128)S(1)}, s32[]{:T(128)}, bf16[1,12,1024,64]{3,2,1,0:T(8,128)(2,1)}, bf16[1,12,4096,64]{3,2,1,0:T(8,128)(2,1)}, ...), branch_computations={%region_29.31_spmd, %region_32.34_spmd, %region_35.37_spmd, %regio... | conditional | flops 2081166848 | bytes 143756960 | solution.py:220
  824.8 29.7 %conditional.5 = (bf16[1,1024,64]{1,2,0:T(8,128)(2,1)}, bf16[1,4096,64]{1,2,0:T(8,128)(2,1)}, bf16[1,4096,64]{1,2,0:T(8,128)(2,1)}) conditional(s32[]{:T(128)} %get-tuple-element.1366, (s32[1,1024]{1,0:T(1,128)S(1)}, s32[]{:T(128)}, bf16[1,12,1024,64]{3,2,1,0:T(8,128)(2,1)}, bf16[1,12,4096,64]{3,2,1,0:T(8,128)(2,1)}, ...), branch_computations={%region_29.31_spmd, %region_32.34_spmd, %region_35.37_spmd, %regio... | conditional | flops 2081166848 | bytes 143756960 | solution.py:220
  860.3 29.7 %conditional.5 = (bf16[1,1024,64]{1,2,0:T(8,128)(2,1)}, bf16[1,4096,64]{1,2,0:T(8,128)(2,1)}, bf16[1,4096,64]{1,2,0:T(8,128)(2,1)}) conditional(s32[]{:T(128)} %get-tuple-element.1366, (s32[1,1024]{1,0:T(1,128)S(1)}, s32[]{:T(128)}, bf16[1,12,1024,64]{3,2,1,0:T(8,128)(2,1)}, bf16[1,12,4096,64]{3,2,1,0:T(8,128)(2,1)}, ...), branch_computations={%region_29.31_spmd, %region_32.34_spmd, %region_35.37_spmd, %regio... | conditional | flops 2081166848 | bytes 143756960 | solution.py:220
  901.5 11.2 convert_element_type.251
  912.7 9.5 copy.108
  922.3 11.2 convert_element_type.255
  933.4 9.5 copy.109
  948.6 10.8 fusion.210
  960.8 10.2 fusion.196
  971.0 847.5 %reduce-scatter.7.cloned.1.call-done = bf16[1024,768]{0,1:T(8,128)(2,1)} async-done(((bf16[4096,768]{0,1:T(8,128)(2,1)}), bf16[1024,768]{0,1:T(8,128)(2,1)}) %reduce-scatter.7.cloned.1.call-update) | async-done | bytes 1572880 | tf_op jit(solution)/shard_map/reduce_scatter | solution.py:232
  1818.6 61.1 %reduce-scatter.9.cloned.1.call-done = bf16[1024,768]{0,1:T(8,128)(2,1)} async-done(((bf16[4096,768]{0,1:T(8,128)(2,1)}), bf16[1024,768]{0,1:T(8,128)(2,1)}) %reduce-scatter.9.cloned.1.call-update) | async-done | bytes 1572880 | tf_op jit(solution)/shard_map/reduce_scatter | solution.py:235
  1879.7 9.0 fusion.194
  1889.4 10.3 fusion.199
  1926.7 41.1 %all-reduce.14 = (f32[768]{0:T(1024)}, f32[768]{0:T(1024)}, f32[768]{0:T(1024)}, f32[768]{0:T(1024)}, f32[768]{0:T(1024)}, /*index=5*/f32[768]{0:T(1024)}, f32[7...) all-reduce(f32[768]{0:T(1024)S(1)} %reduce_sum.365, ...), channel_id=1, replica_groups=mesh['seq'=8,'pass'=4] {'seq','pass'}, use_global_device_ids=true, to_apply=%region_48.49 | all-reduce | flops 12288 | bytes 98304 | tf_op jit(solution)/shard_map/psum | solution.py:267
  1968.4 16.3 reduce-scatter.13.cloned.1.call-done
  1984.7 141.8 %reduce-scatter.15.cloned.1.call-done = f32[24,3072]{1,0:T(8,128)} async-done(((f32[768,3072]{1,0:T(8,128)}), f32[24,3072]{1,0:T(8,128)}) %reduce-scatter.15.cloned.1.call-update) | async-done | bytes 294928 | tf_op jit(solution)/shard_map/reduce_scatter | solution.py:253
  2126.5 141.0 %reduce-scatter.17.cloned.1.call-done = f32[96,768]{1,0:T(8,128)} async-done(((f32[3072,768]{1,0:T(8,128)}), f32[96,768]{1,0:T(8,128)}) %reduce-scatter.17.cloned.1.call-update) | async-done | bytes 294928 | tf_op jit(solution)/shard_map/reduce_scatter | solution.py:254
  2267.5 125.5 %reduce-scatter.11.cloned.1.call-done = f32[24,2304]{1,0:T(8,128)} async-done(((f32[768,2304]{1,0:T(8,128)}), f32[24,2304]{1,0:T(8,128)}) %reduce-scatter.11.cloned.1.call-update) | async-done | bytes 221200 | tf_op jit(solution)/shard_map/reduce_scatter | solution.py:251
  (938 shorter events, 644.1 us)
Async XLA Ops:
  7.2 66.5 %all-gather.7.cloned.1.call-start = ((), (), s32[]{:S(2)}) async-start(), calls=%async_computation.6 | async-start | bytes 3649536 | tf_op jit(solution)/shard_map/all_gather | solution.py:84
  7.9 121.8 %all-gather.11.cloned.1.call-start = ((), (), s32[]{:S(2)}) async-start(), calls=%async_computation.8 | async-start | bytes 7864320 | tf_op jit(solution)/shard_map/all_gather | solution.py:99
  8.0 65.7 %copy-start.41 = (f32[768]{0:T(1024)S(1)}, f32[768]{0:T(1024)}, u32[]{:S(2)}) copy-start(f32[768]{0:T(1024)} %param.101) | copy-start | bytes 9220
  8.0 65.7 %copy-start.61 = (f32[768]{0:T(1024)S(1)}, f32[768]{0:T(1024)}, u32[]{:S(2)}) copy-start(f32[768]{0:T(1024)} %param.102) | copy-start | bytes 9220
  9.7 70.5 %copy-start.16 = (bf16[1,1024,768]{1,2,0:T(8,128)(2,1)}, bf16[1,1024,768]{1,2,0:T(8,128)(2,1)S(1)}, u32[]{:S(2)}) copy-start(bf16[1,1024,768]{1,2,0:T(8,128)(2,1)S(1)} %copy.66) | copy-start | bytes 4718596
  9.8 63.9 %copy-start.35 = (f32[768]{0:T(1024)}, f32[768]{0:T(1024)S(1)}, u32[]{:S(2)}) copy-start(f32[768]{0:T(1024)S(1)} %dynamic-slice_reduce_fusion) | copy-start | bytes 9220
  10.2 70.0 %copy-start.37 = (f32[1024]{0:T(1024)}, f32[1024]{0:T(1024)S(1)}, u32[]{:S(2)}) copy-start(f32[1024]{0:T(1024)S(1)} %broadcast_multiply_fusion.2) | copy-start | bytes 12292
  10.8 69.4 %copy-start.47 = (f32[1024]{0:T(1024)}, f32[1024]{0:T(1024)S(1)}, u32[]{:S(2)}) copy-start(f32[1024]{0:T(1024)S(1)} %fusion.191) | copy-start | bytes 12292
  10.8 69.4 %copy-start.43 = (f32[1024]{0:T(1024)}, f32[1024]{0:T(1024)S(1)}, u32[]{:S(2)}) copy-start(f32[1024]{0:T(1024)S(1)} %fusion.205) | copy-start | bytes 12292
  10.8 69.4 %copy-start.54 = (f32[768]{0:T(1024)S(1)}, f32[768]{0:T(1024)}, u32[]{:S(2)}) copy-start(f32[768]{0:T(1024)} %param.105) | copy-start | bytes 9220
  10.8 69.4 %copy-start.55 = (f32[768]{0:T(1024)S(1)}, f32[768]{0:T(1024)}, u32[]{:S(2)}) copy-start(f32[768]{0:T(1024)} %param.104) | copy-start | bytes 9220
  84.4 93.3 %all-gather.9.cloned.1.call-start = ((), (), s32[]{:S(2)}) async-start(), calls=%async_computation.7 | async-start | bytes 7864320 | tf_op jit(solution)/shard_map/all_gather | solution.py:98
  87.8 279.6 %all-gather.13.cloned.1.call-start = ((), (), s32[]{:S(2)}) async-start(), calls=%async_computation.9 | async-start | bytes 1216512 | tf_op jit(solution)/shard_map/all_gather | solution.py:85
  88.4 283.6 %all-gather.15.cloned.1.call-start = ((), (), s32[]{:S(2)}) async-start(), calls=%async_computation.10 | async-start | bytes 4866048 | tf_op jit(solution)/shard_map/all_gather | solution.py:86
  88.9 321.7 %all-gather.17.cloned.1.call-start = ((), (), s32[]{:S(2)}) async-start(), calls=%async_computation.11 | async-start | bytes 4866048 | tf_op jit(solution)/shard_map/all_gather | solution.py:87
  89.5 1729.0 %reduce-scatter.7.cloned.1.call-start = ((), (), s32[]{:S(2)}) async-start(), calls=%async_computation.12 | async-start | bytes 7864320 | tf_op jit(solution)/shard_map/reduce_scatter | solution.py:232
  197.7 14.7 copy-start.24
  371.4 76.8 %copy-start.20 = (f32[1024,768]{0,1:T(8,128)}, f32[1024,768]{0,1:T(8,128)S(1)}, u32[]{:S(2)}) copy-start(f32[1024,768]{0,1:T(8,128)S(1)} %get-tuple-element.1126) | copy-start | bytes 9437188
  371.5 76.8 %copy-start.39 = (f32[1024]{0:T(1024)}, f32[1024]{0:T(1024)S(1)}, u32[]{:S(2)}) copy-start(f32[1024]{0:T(1024)S(1)} %broadcast_multiply_fusion.1) | copy-start | bytes 12292
  371.9 76.4 %copy-start.45 = (f32[1024]{0:T(1024)}, f32[1024]{0:T(1024)S(1)}, u32[]{:S(2)}) copy-start(f32[1024]{0:T(1024)S(1)} %fusion.206) | copy-start | bytes 12292
  470.1 6.3 copy-start.13
  520.0 6.3 copy-start.13
  555.8 6.3 copy-start.13
  591.2 6.3 copy-start.13
  626.7 6.3 copy-start.13
  662.2 6.3 copy-start.13
  697.6 6.3 copy-start.13
  733.1 6.3 copy-start.13
  768.5 6.3 copy-start.13
  803.9 6.3 copy-start.13
  839.4 6.3 copy-start.13
  874.9 6.3 copy-start.13
  922.2 957.4 %reduce-scatter.9.cloned.1.call-start = ((), (), s32[]{:S(2)}) async-start(), calls=%async_computation.13 | async-start | bytes 7864320 | tf_op jit(solution)/shard_map/reduce_scatter | solution.py:235
  942.9 5.6 copy-start.21
  942.9 5.6 copy-start.40
  943.0 5.6 copy-start.46
  943.0 1041.7 %reduce-scatter.13.cloned.1.call-start = ((), (), s32[]{:S(2)}) async-start(), calls=%async_computation.15 | async-start | bytes 2433024 | tf_op jit(solution)/shard_map/reduce_scatter | solution.py:252
  948.5 1178.0 %reduce-scatter.15.cloned.1.call-start = ((), (), s32[]{:S(2)}) async-start(), calls=%async_computation.16 | async-start | bytes 9732096 | tf_op jit(solution)/shard_map/reduce_scatter | solution.py:253
  959.4 1308.1 %reduce-scatter.17.cloned.1.call-start = ((), (), s32[]{:S(2)}) async-start(), calls=%async_computation.17 | async-start | bytes 9732096 | tf_op jit(solution)/shard_map/reduce_scatter | solution.py:254
  970.9 908.7 %copy-start.17 = (bf16[1,1024,768]{1,2,0:T(8,128)(2,1)S(1)}, bf16[1,1024,768]{1,2,0:T(8,128)(2,1)}, u32[]{:S(2)}) copy-start(bf16[1,1024,768]{1,2,0:T(8,128)(2,1)} %copy-done.16) | copy-start | bytes 4718596
  970.9 908.7 %copy-start.32 = (bf16[12,1024,64]{1,2,0:T(8,128)(2,1)S(1)}, bf16[12,1024,64]{1,2,0:T(8,128)(2,1)}, u32[]{:S(2)}) copy-start(bf16[12,1024,64]{1,2,0:T(8,128)(2,1)} %get-tuple-element.909) | copy-start | bytes 4718596
  970.9 908.7 %copy-start.36 = (f32[768]{0:T(1024)S(1)}, f32[768]{0:T(1024)}, u32[]{:S(2)}) copy-start(f32[768]{0:T(1024)} %copy-done.35) | copy-start | bytes 9220
  970.9 908.7 %copy-start.38 = (f32[1024]{0:T(1024)S(1)}, f32[1024]{0:T(1024)}, u32[]{:S(2)}) copy-start(f32[1024]{0:T(1024)} %copy-done.37) | copy-start | bytes 12292
  970.9 908.7 %copy-start.42 = (f32[768]{0:T(1024)S(1)}, f32[768]{0:T(1024)}, u32[]{:S(2)}) copy-start(f32[768]{0:T(1024)} %param.101) | copy-start | bytes 9220
  970.9 908.7 %copy-start.44 = (f32[1024]{0:T(1024)S(1)}, f32[1024]{0:T(1024)}, u32[]{:S(2)}) copy-start(f32[1024]{0:T(1024)} %copy-done.43) | copy-start | bytes 12292
  971.0 908.7 %copy-start.62 = (f32[768]{0:T(1024)S(1)}, f32[768]{0:T(1024)}, u32[]{:S(2)}) copy-start(f32[768]{0:T(1024)} %param.102) | copy-start | bytes 9220
  971.0 1422.0 %reduce-scatter.11.cloned.1.call-start = ((), (), s32[]{:S(2)}) async-start(), calls=%async_computation.14 | async-start | bytes 7299072 | tf_op jit(solution)/shard_map/reduce_scatter | solution.py:251
  1922.6 470.4 %copy-start.1 = (f32[4,768]{1,0:T(4,128)S(1)}, f32[4,768]{1,0:T(4,128)}, u32[]{:S(2)}) copy-start(f32[4,768]{1,0:T(4,128)} %param.100) | copy-start | bytes 36868
  (118 other events, 283.9 us)
Sparse Core Ops, SparseCore 0:
  10.9 62.7 all-gather.6
  84.5 45.1 all-gather.10
  131.3 46.3 all-gather.8
  180.5 54.0 all-gather.12
  237.3 62.5 all-gather.14
  302.7 62.5 all-gather.16
  922.3 896.1 reduce-scatter.6
  1821.3 58.3 reduce-scatter.8
  1885.5 99.1 reduce-scatter.12
  1992.0 134.4 reduce-scatter.14
  2133.0 134.4 reduce-scatter.16
  2274.5 118.4 reduce-scatter.10
where the time goes:
time: 2420 us; the launch traced here: 2400 us
  waiting for transfers between devices  1450 us (60%)
  local copies, waits for them, and re-layouts  426 us (18%)
  matrix products  328 us (14%)
  loops' own time  81.3 us (3%)
  other arithmetic  60.7 us (3%)
  blocking collectives  41.1 us (2%)
    reduce_scatter x1, waiting for transfers between devices, per_device(): lax.psum_scatter(whole_rows(key_grads).astype(jnp.bfloat16), 'pass', scat...  848 us
    reduce_scatter x1, waiting for transfers between devices, per_device(): lax.psum_scatter(up_grad, ('seq', 'pass'), scatter_dimension=0, tiled=True)  142 us
    reduce_scatter x1, waiting for transfers between devices, per_device(): lax.psum_scatter(down_grad, ('seq', 'pass'), scatter_dimension=0, tiled=T...  141 us
    dot_general x76, matrix products, matmul_nt(): lax.dot_general(first_op, second_op, (((1,), (1,)), ((), ())), preferred_...  140 us
    reduce_scatter x1, waiting for transfers between devices, per_device(): lax.psum_scatter(qkv_grad, ('seq', 'pass'), scatter_dimension=0, tiled=True)  126 us
    dot_general x52, matrix products, matmul(): return jnp.dot(first_op, second_op, preferred_element_type=jnp.float32)  102 us
    dot_general x52, matrix products, matmul_tn(): lax.dot_general(first_op, second_op, (((0,), (0,)), ((), ())), preferred_...  85.9 us
    all_gather x1, waiting for transfers between devices, per_device(): lax.all_gather(w_qkv, ('seq', 'pass'), axis=0, tiled=True)  62.9 us
  transfers between devices with their start and end apart: 12, of which 9 were waited for; matrix products, arithmetic and copies ran while one was open for 14% of the time, Pallas kernels for 0%

commit v1 on v0

v1 whole, which is shorter than its diff:
```python
import functools

import jax
import jax.numpy as jnp
from jax import lax
from jax.experimental import pallas as pl
from jax.experimental.pallas import tpu as pltpu
from jax.sharding import PartitionSpec as P

HEADS = 12
HEAD_DIM = 64
LANES = 128
NORM_EPS = 1e-05
MASKED = -1e30
BIAS_COL = 64
STAT_COL = 65
DELTA_COL = 64

bfloat = jnp.bfloat16
single = jnp.float32


def dot_nn(a, b):
    return jnp.dot(a, b, preferred_element_type=single)


def dot_nt(a, b):
    return lax.dot_general(a, b, (((1,), (1,)), ((), ())), preferred_element_type=single)


def dot_tn(a, b):
    return lax.dot_general(a, b, (((0,), (0,)), ((), ())), preferred_element_type=single)


def three_parts(value):
    first = value.astype(bfloat).astype(single)
    rest = value - first
    second = rest.astype(bfloat).astype(single)
    return first, second, rest - second


def with_columns(base, start, columns):
    lane = lax.broadcasted_iota(jnp.int32, base.shape, 1)
    for offset, column in enumerate(columns):
        base = jnp.where(lane == start + offset, column, base)
    return base


def norm_parts(values):
    center = values - jnp.mean(values, axis=-1, keepdims=True)
    inverse = lax.rsqrt(jnp.mean(center * center, axis=-1, keepdims=True) + NORM_EPS)
    return center * inverse, inverse


def norm_back(grad, gain, normed, inverse):
    scaled = grad * gain
    mean_one = jnp.mean(scaled, axis=-1, keepdims=True)
    mean_two = jnp.mean(scaled * normed, axis=-1, keepdims=True)
    return inverse * (scaled - mean_one - normed * mean_two)


def head_slab(packed, index):
    low = (index // 2) * LANES
    slab = packed[:, low : low + LANES]
    if index % 2:
        slab = pltpu.roll(slab, HEAD_DIM, axis=1)
    return slab


def pack_heads(slabs):
    packed = []
    lane = lax.broadcasted_iota(jnp.int32, slabs[0].shape, 1)
    for index in range(0, len(slabs), 2):
        if index + 1 < len(slabs):
            other = pltpu.roll(slabs[index + 1], HEAD_DIM, axis=1)
            packed.append(jnp.where(lane < HEAD_DIM, slabs[index], other))
        else:
            packed.append(slabs[index])
    width = len(slabs) * HEAD_DIM
    return jnp.concatenate(packed, axis=1)[:, :width]


def project_kernel(heads, count, me_ref, *refs):
    pieces = refs[:count]
    pass_ref, gain_ref, shift_ref, weight_ref, bias_ref, depth_ref = refs[count : count + 6]
    q_ref, k_ref, v_ref = refs[-3:]
    slot = pl.program_id(0)
    pass_index = me_ref[1 + slot]
    pass_row = pass_ref[pl.ds(pass_index, 1), :]
    rows = pieces[0][...]
    for index in range(1, count):
        rows = jnp.where(slot == index, pieces[index][...], rows)
    normed, _ = norm_parts(rows.astype(single) + pass_row)
    low = (normed * gain_ref[...] + shift_ref[...]).astype(bfloat)
    projected = dot_nn(low, weight_ref[...]) + bias_ref[...]
    lane = lax.broadcasted_iota(jnp.int32, (low.shape[0], LANES), 1)
    inside = lane < HEAD_DIM
    depth_bias = jnp.where(pass_index < depth_ref[...], 0.0, MASKED)
    q_rest = jnp.where(lane == BIAS_COL, 1.0, 0.0)
    k_rest = jnp.where(
        lane == BIAS_COL, depth_bias, jnp.where((lane >= STAT_COL) & (lane < STAT_COL + 3), 1.0, 0.0)
    )
    v_rest = jnp.where((lane >= DELTA_COL) & (lane < DELTA_COL + 3), 1.0, 0.0)
    for head in range(heads):
        q_part = head_slab(projected, head).astype(bfloat).astype(single) * (HEAD_DIM**-0.5)
        q_ref[head] = jnp.where(inside, q_part, q_rest).astype(bfloat)
        k_ref[head] = jnp.where(inside, head_slab(projected, heads + head), k_rest).astype(bfloat)
        v_ref[head] = jnp.where(inside, head_slab(projected, 2 * heads + head), v_rest).astype(bfloat)


def project(order, pieces, passes, pass_emb, gain, shift, weight, bias, depth, previous):
    count = len(pieces)
    length, width = pieces[0].shape
    heads = weight.shape[1] // (3 * HEAD_DIM)
    block = min(512, length)
    steps = length // block

    def piece_spec(index):
        def where(slot, step, order_ref):
            return (jnp.where(slot == index, step, jnp.where(slot < index, 0, steps - 1)), 0)

        return pl.BlockSpec((block, width), where)

    def whole(shape):
        return pl.BlockSpec(shape, lambda slot, step, order_ref: (0,) * len(shape))

    out_spec = pl.BlockSpec(
        (heads, pl.Squeezed(), block, LANES),
        lambda slot, step, order_ref: (0, order_ref[1 + slot], step, 0),
    )
    shape = jax.ShapeDtypeStruct((heads, passes, length, LANES), bfloat)
    in_specs = [piece_spec(index) for index in range(count)] + [
        whole(pass_emb.shape),
        whole(gain.shape),
        whole(shift.shape),
        whole(weight.shape),
        whole(bias.shape),
        pl.BlockSpec((block, 1), lambda slot, step, order_ref: (step, 0)),
    ]
    operands = [*pieces, pass_emb, gain, shift, weight, bias, depth]
    aliases = {}
    if previous is not None:
        aliases = {1 + len(operands) + index: index for index in range(3)}
        in_specs += [pl.BlockSpec(memory_space=pl.ANY)] * 3
        operands += list(previous)
    return pl.pallas_call(
        functools.partial(project_kernel, heads, count),
        grid_spec=pltpu.PrefetchScalarGridSpec(
            num_scalar_prefetch=1,
            grid=(count, steps),
            in_specs=in_specs,
            out_specs=[out_spec] * 3,
        ),
        out_shape=[shape] * 3,
        input_output_aliases=aliases,
        compiler_params=pltpu.CompilerParams(vmem_limit_bytes=40 << 20),
        name="project",
    )(order, *operands)


def attend_kernel(passes, block, q_ref, k_ref, v_ref, out_ref, q_next_ref, held):
    heads = q_ref.shape[0]
    blocks = k_ref.shape[2] // block
    step = pl.program_id(0)
    row = lax.broadcasted_iota(jnp.int32, (block, block), 0)
    col = lax.broadcasted_iota(jnp.int32, (block, block), 1)
    causal = col <= row

    def one_head(head, count):
        for query_pass in range(passes):
            query = q_ref[head, query_pass]
            highest = None
            kept = []
            for key_pass in range(query_pass + 1):
                for tile in range(count):
                    scores = dot_nt(query, k_ref[head, key_pass, tile * block : (tile + 1) * block, :])
                    if tile == count - 1:
                        scores = jnp.where(causal, scores, MASKED)
                    kept.append(scores)
                    for lane in range(0, block, LANES):
                        part = scores[:, lane : lane + LANES]
                        highest = part if highest is None else jnp.maximum(highest, part)
            highest = jnp.max(highest, axis=-1, keepdims=True)
            total = None
            for index, scores in enumerate(kept):
                key_pass, tile = divmod(index, count)
                weights = jnp.exp(scores - highest).astype(bfloat)
                term = dot_nn(weights, v_ref[head, key_pass, tile * block : (tile + 1) * block, :])
                total = term if total is None else total + term
            row_sum = total[:, DELTA_COL : DELTA_COL + 1]
            log_sum = highest + jnp.log(row_sum)
            q_next_ref[head, query_pass] = with_columns(
                query.astype(single), STAT_COL, three_parts(-log_sum)
            ).astype(bfloat)
            held[head, query_pass] = total * (1.0 / row_sum)

    for index in range(blocks):

        @pl.when(step == index)
        def _():
            lax.fori_loop(0, heads, lambda head, _: (one_head(head, index + 1), 0)[1], 0)

    for query_pass in range(passes):
        out_ref[query_pass] = pack_heads([held[head, query_pass] for head in range(heads)]).astype(bfloat)


def attend(queries, keys, values):
    heads, passes, length, _ = queries.shape
    block = min(256, length)
    whole = pl.BlockSpec(keys.shape, lambda step: (0, 0, 0, 0), pipeline_mode=pl.Buffered(1))
    part = pl.BlockSpec((heads, passes, block, LANES), lambda step: (0, 0, step, 0))
    packed = heads * HEAD_DIM
    return pl.pallas_call(
        functools.partial(attend_kernel, passes, block),
        grid=(length // block,),
        in_specs=[part, whole, whole],
        out_specs=[pl.BlockSpec((passes, block, packed), lambda step: (0, step, 0)), part],
        out_shape=[
            jax.ShapeDtypeStruct((passes, length, packed), bfloat),
            jax.ShapeDtypeStruct(queries.shape, bfloat),
        ],
        scratch_shapes=[pltpu.VMEM((heads, passes, block, LANES), single)],
        compiler_params=pltpu.CompilerParams(vmem_limit_bytes=56 << 20),
        name="attend",
    )(queries, keys, values)


def attend_back_kernel(
    passes, block, me_ref, q_ref, out_ref, k_ref, v_ref, grad_a, grad_b, grad_c, grad_d, all_ref, *scratch
):
    grad_refs = (grad_a, grad_b, grad_c, grad_d)
    key_acc, value_acc, grad_held, query_held = scratch
    heads = q_ref.shape[0]
    blocks = k_ref.shape[2] // block
    step = pl.program_id(0)
    me = me_ref[0]
    row = lax.broadcasted_iota(jnp.int32, (block, block), 0)
    col = lax.broadcasted_iota(jnp.int32, (block, block), 1)
    causal = row <= col
    inside = lax.broadcasted_iota(jnp.int32, (block, LANES), 1) < HEAD_DIM

    @pl.when(step == 0)
    def _():
        key_acc[...] = jnp.zeros(key_acc.shape, single)
        value_acc[...] = jnp.zeros(value_acc.shape, single)

    padded = ((heads * HEAD_DIM + LANES - 1) // LANES) * LANES
    for slot in range(passes):
        query_pass = jnp.bitwise_xor(me, slot)
        grad = grad_refs[slot][...].astype(single)
        out = out_ref[query_pass].astype(single)
        tail = jnp.zeros((block, padded - heads * HEAD_DIM), single)
        if padded > heads * HEAD_DIM:
            grad = jnp.concatenate([grad, tail], axis=1)
            out = jnp.concatenate([out, tail], axis=1)
        product = grad * out
        for head in range(heads):
            delta = jnp.sum(
                jnp.where(inside, head_slab(product, head), 0.0), axis=-1, keepdims=True
            )
            base = jnp.where(inside, head_slab(grad, head), 0.0)
            grad_held[head, query_pass] = with_columns(base, DELTA_COL, three_parts(-delta)).astype(bfloat)

    def one_head(head, count):
        query_sums = [None] * passes
        for key_pass in range(passes):
            span = passes - key_pass
            query = q_ref[head, key_pass:passes].reshape(span * block, LANES)
            grad = grad_held[head, key_pass:passes].reshape(span * block, LANES)
            for tile in range(count):
                window = slice(tile * block, (tile + 1) * block)
                key = k_ref[head, key_pass, window, :]
                value = v_ref[head, key_pass, window, :]
                prob = jnp.exp(dot_nt(key, query))
                if tile == count - 1:
                    prob = jnp.where(jnp.concatenate([causal] * span, axis=1), prob, 0.0)
                value_acc[head, key_pass, window, :] += dot_nn(prob.astype(bfloat), grad)
                score_grad = (prob * dot_nt(value, grad)).astype(bfloat)
                key_acc[head, key_pass, window, :] += dot_nn(score_grad, query)
                term = dot_tn(key, score_grad)
                for query_pass in range(key_pass, passes):
                    first = (query_pass - key_pass) * block
                    part = term[:, first : first + block]
                    old = query_sums[query_pass]
                    query_sums[query_pass] = part if old is None else old + part
        for query_pass in range(passes):
            query_held[head, query_pass] = query_sums[query_pass].T * (HEAD_DIM**-0.5)

    for index in range(blocks):

        @pl.when(step == blocks - 1 - index)
        def _():
            lax.fori_loop(0, heads, lambda head, _: (one_head(head, index + 1), 0)[1], 0)
            window = slice(index * block, (index + 1) * block)
            for query_pass in range(passes):
                slabs = [query_held[head, query_pass] for head in range(heads)]
                slabs += [key_acc[head, query_pass, window, :] for head in range(heads)]
                slabs += [value_acc[head, query_pass, window, :] for head in range(heads)]
                all_ref[query_pass] = pack_heads(slabs).astype(bfloat)


def attend_back(me, queries, outs, keys, values, grads):
    heads, passes, length, _ = queries.shape
    block = min(256, length)
    steps = length // block
    packed = heads * HEAD_DIM
    whole = pl.BlockSpec(keys.shape, lambda step, me_ref: (0, 0, 0, 0), pipeline_mode=pl.Buffered(1))
    part = pl.BlockSpec((heads, passes, block, LANES), lambda step, me_ref: (0, 0, steps - 1 - step, 0))
    return pl.pallas_call(
        functools.partial(attend_back_kernel, passes, block),
        grid_spec=pltpu.PrefetchScalarGridSpec(
            num_scalar_prefetch=1,
            grid=(steps,),
            in_specs=[
                part,
                pl.BlockSpec((passes, block, packed), lambda step, me_ref: (0, steps - 1 - step, 0)),
                whole,
                whole,
            ]
            + [pl.BlockSpec((block, packed), lambda step, me_ref: (steps - 1 - step, 0))] * passes,
            out_specs=pl.BlockSpec(
                (passes, block, 3 * packed), lambda step, me_ref: (0, steps - 1 - step, 0)
            ),
            scratch_shapes=[
                pltpu.VMEM(keys.shape, single),
                pltpu.VMEM(keys.shape, single),
                pltpu.VMEM((heads, passes, block, LANES), bfloat),
                pltpu.VMEM((heads, passes, block, LANES), single),
            ],
        ),
        out_shape=jax.ShapeDtypeStruct((passes, length, 3 * packed), bfloat),
        compiler_params=pltpu.CompilerParams(vmem_limit_bytes=60 << 20),
        name="attend_back",
    )(me, queries, outs, keys, values, *grads)


def middle_kernel(groups, chunks, me_ref, *refs):
    parts = refs[:groups]
    (
        x_ref,
        cot_ref,
        pass_ref,
        w_out_ref,
        w_up_ref,
        w_down_ref,
        out_bias_ref,
        gain_ref,
        shift_ref,
        up_bias_ref,
        down_bias_ref,
    ) = refs[groups : groups + 11]
    outs = refs[groups + 11 :]
    rows_ref, mixed_grad_ref, normed_ref, active_ref, upper_ref, proj_ref, sums_ref, up_sum_ref = outs[:8]
    grads = outs[8:]
    me = me_ref[0]
    width = x_ref.shape[1]
    packed = width // groups
    step = pl.program_id(0)

    def group_window(slot):
        start = pl.multiple_of(jnp.bitwise_xor(me, slot) * packed, packed)
        return pl.ds(start, packed)

    mixed = x_ref[...].astype(single) + pass_ref[...] + out_bias_ref[...]
    for slot in range(groups):
        mixed += dot_nn(parts[slot][...], w_out_ref[group_window(slot), :])
    normed, inverse = norm_parts(mixed)
    low = (normed * gain_ref[...] + shift_ref[...]).astype(bfloat)
    normed_ref[...] = low
    down_low = cot_ref[...]
    out_grad = down_low.astype(single)
    total = mixed + down_bias_ref[...]
    back = jnp.zeros_like(mixed)
    hidden = w_up_ref.shape[1]
    size = hidden // chunks
    up_sums = []
    for chunk in range(chunks):
        window = slice(chunk * size, (chunk + 1) * size)
        upper = dot_nn(low, w_up_ref[:, window]) + up_bias_ref[:, window]
        below = 0.5 + 0.5 * lax.erf(upper * (0.5**0.5))
        density = jnp.exp(-0.5 * upper * upper) * 0.3989422804014327
        active = (upper * below).astype(bfloat)
        active_ref[:, window] = active
        total += dot_nn(active, w_down_ref[window, :])
        grad = dot_nt(down_low, w_down_ref[window, :]) * (below + upper * density)
        upper_low = grad.astype(bfloat)
        upper_ref[:, window] = upper_low
        up_sums.append(jnp.sum(upper_low.astype(single), axis=0, keepdims=True))
        back += dot_nt(upper_low, w_up_ref[:, window])
    rows_ref[...] = total.astype(bfloat)
    mixed_grad = out_grad + norm_back(back, gain_ref[...], normed, inverse)
    mixed_grad_ref[...] = mixed_grad
    proj_low = mixed_grad.astype(bfloat)
    proj_ref[...] = proj_low
    for slot in range(groups):
        grads[slot][...] = dot_nt(proj_low, w_out_ref[group_window(slot), :]).astype(bfloat)

    @pl.when(step == 0)
    def _():
        sums_ref[...] = jnp.zeros(sums_ref.shape, single)
        up_sum_ref[...] = jnp.zeros(up_sum_ref.shape, single)

    def column_sum(values):
        return jnp.sum(values, axis=0, keepdims=True)

    sums_ref[0:1, :] += column_sum(mixed_grad)
    sums_ref[1:2, :] += column_sum(back * normed)
    sums_ref[2:3, :] += column_sum(back)
    sums_ref[3:4, :] += column_sum(out_grad)
    up_sum_ref[...] += jnp.concatenate(up_sums, axis=1)


def middle(me, parts, x_own, cot, pass_row, w_out, w_up, w_down, out_bias, gain, shift, up_bias, down_bias):
    length, width = x_own.shape
    hidden = w_up.shape[1]
    groups = len(parts)
    packed = width // groups
    block = min(256, length)

    def rows(size):
        return pl.BlockSpec((block, size), lambda step, me_ref: (step, 0))

    def whole(shape):
        return pl.BlockSpec(shape, lambda step, me_ref: (0, 0), pipeline_mode=pl.Buffered(1))

    def fixed(shape):
        return pl.BlockSpec(shape, lambda step, me_ref: (0, 0))

    struct = jax.ShapeDtypeStruct
    operands = (x_own, cot, pass_row, w_out, w_up, w_down, out_bias, gain, shift, up_bias, down_bias)
    return pl.pallas_call(
        functools.partial(middle_kernel, groups, 4),
        grid_spec=pltpu.PrefetchScalarGridSpec(
            num_scalar_prefetch=1,
            grid=(length // block,),
            in_specs=[rows(packed)] * groups
            + [rows(width), rows(width)]
            + [whole(operand.shape) for operand in operands[2:]],
            out_specs=[
                rows(width),
                rows(width),
                rows(width),
                rows(hidden),
                rows(hidden),
                rows(width),
                fixed((8, width)),
                fixed((1, hidden)),
            ]
            + [rows(packed)] * groups,
        ),
        out_shape=[
            struct((length, width), bfloat),
            struct((length, width), single),
            struct((length, width), bfloat),
            struct((length, hidden), bfloat),
            struct((length, hidden), bfloat),
            struct((length, width), bfloat),
            struct((8, width), single),
            struct((1, hidden), single),
        ]
        + [struct((length, packed), bfloat)] * groups,
        compiler_params=pltpu.CompilerParams(vmem_limit_bytes=60 << 20),
        name="middle",
    )(me, *parts, *operands)


def project_back_kernel(count, me_ref, *refs):
    pieces = refs[:count]
    pass_ref, gain_ref, shift_ref, weight_ref, grad_ref = refs[count : count + 5]
    rows_ref, weight_grad_ref, sums_ref, bias_ref, pass_sum_ref = refs[count + 5 :]
    slot = pl.program_id(0)
    step = pl.program_id(1)
    pass_index = me_ref[1 + slot]
    rows = pieces[0][...]
    for index in range(1, count):
        rows = jnp.where(slot == index, pieces[index][...], rows)
    normed, inverse = norm_parts(rows.astype(single) + pass_ref[pl.ds(pass_index, 1), :])
    low = (normed * gain_ref[...] + shift_ref[...]).astype(bfloat)
    grad = grad_ref[...]
    back = dot_nt(grad, weight_ref[...])
    part = norm_back(back, gain_ref[...], normed, inverse)
    rows_ref[...] = part.astype(bfloat)

    def column_sum(values):
        return jnp.sum(values, axis=0, keepdims=True)

    @pl.when((slot == 0) & (step == 0))
    def _():
        weight_grad_ref[...] = jnp.zeros(weight_grad_ref.shape, single)
        sums_ref[...] = jnp.zeros(sums_ref.shape, single)
        bias_ref[...] = jnp.zeros(bias_ref.shape, single)
        pass_sum_ref[...] = jnp.zeros(pass_sum_ref.shape, single)

    weight_grad_ref[...] += dot_tn(low, grad)
    sums_ref[0:1, :] += column_sum(back * normed)
    sums_ref[1:2, :] += column_sum(back)
    bias_ref[...] += column_sum(grad.astype(single))
    pass_sum_ref[pl.ds(pass_index, 1), :] += column_sum(part)


def project_back(order, pieces, pass_emb, gain, shift, weight, grads):
    count = len(pieces)
    length, width = pieces[0].shape
    passes, _, packed = grads.shape
    block = min(512, length)
    steps = length // block

    def piece_spec(index):
        def where(slot, step, order_ref):
            return (jnp.where(slot == index, step, jnp.where(slot < index, 0, steps - 1)), 0)

        return pl.BlockSpec((block, width), where)

    def whole(shape):
        return pl.BlockSpec(shape, lambda slot, step, order_ref: (0,) * len(shape))

    struct = jax.ShapeDtypeStruct
    return pl.pallas_call(
        functools.partial(project_back_kernel, count),
        grid_spec=pltpu.PrefetchScalarGridSpec(
            num_scalar_prefetch=1,
            grid=(count, steps),
            in_specs=[piece_spec(index) for index in range(count)]
            + [
                whole(pass_emb.shape),
                whole(gain.shape),
                whole(shift.shape),
                whole(weight.shape),
                pl.BlockSpec(
                    (pl.Squeezed(), block, packed),
                    lambda slot, step, order_ref: (order_ref[1 + slot], step, 0),
                ),
            ],
            out_specs=[
                pl.BlockSpec((pl.Squeezed(), block, width), lambda slot, step, order_ref: (slot, step, 0)),
                whole((width, packed)),
                whole((8, width)),
                whole((1, packed)),
                whole((passes, width)),
            ],
        ),
        out_shape=[
            struct((passes, length, width), bfloat),
            struct((width, packed), single),
            struct((8, width), single),
            struct((1, packed), single),
            struct((passes, width), single),
        ],
        compiler_params=pltpu.CompilerParams(vmem_limit_bytes=48 << 20),
        name="project_back",
    )(order, *pieces, pass_emb, gain, shift, weight, grads)


def per_device(
    x_rows,
    pass_depth,
    cotangent,
    pass_emb,
    ln1_gain,
    ln1_bias,
    w_qkv,
    q_bias,
    v_bias,
    w_out,
    out_bias,
    ln2_gain,
    ln2_bias,
    w_up,
    up_bias,
    w_down,
    down_bias,
):
    everyone = ("seq", "pass")
    _, length, width = x_rows.shape
    hidden = w_up.shape[1]
    passes = lax.axis_size("pass")
    devices = passes * lax.axis_size("seq")
    shard = w_qkv.shape[0]
    group = width // passes
    group_heads = group // HEAD_DIM
    me = lax.axis_index("pass")
    order = jnp.concatenate([me[None], jnp.bitwise_xor(me, jnp.arange(passes))]).astype(jnp.int32)

    def swap(value, distance):
        return lax.ppermute(value, "pass", [(k, k ^ distance) for k in range(passes)])

    x_own = x_rows[0]
    x_one = swap(x_own, 1)
    x_two = swap(x_own, 2)
    x_three = swap(x_two, 1)

    by_group = w_qkv.reshape(shard, 3, passes, group).transpose(2, 0, 1, 3).reshape(passes, shard, 3 * group)
    by_rows = lax.all_to_all(by_group, "pass", 0, 0, tiled=True).reshape(passes * shard, 3 * group)
    w_heads = lax.all_gather(by_rows, "seq", axis=0, tiled=True)

    down_cols = w_down.reshape(passes, shard, width).transpose(1, 0, 2).reshape(shard, hidden)
    gathered = lax.all_gather(
        jnp.concatenate([w_out, w_up, down_cols], axis=1), everyone, axis=0, tiled=True
    )
    full_out = gathered[:, :width]
    full_up = gathered[:, width : width + hidden]
    full_down = (
        gathered[:, width + hidden :]
        .reshape(devices, shard, hidden // width, width)
        .transpose(0, 2, 1, 3)
        .reshape(hidden, width)
    )

    gain_one, shift_one = ln1_gain[None], ln1_bias[None]
    own_q_bias = lax.dynamic_slice_in_dim(q_bias, me * group, group)
    own_v_bias = lax.dynamic_slice_in_dim(v_bias, me * group, group)
    bias_row = jnp.concatenate([own_q_bias, jnp.zeros((group,), single), own_v_bias])[None]
    pad = (-3 * group) % LANES
    w_wide = jnp.pad(w_heads, ((0, 0), (0, pad)))
    bias_wide = jnp.pad(bias_row, ((0, 0), (0, pad)))
    depth = pass_depth.reshape(length, 1)
    near = project(
        order[:3], (x_own, x_one), passes, pass_emb, gain_one, shift_one, w_wide, bias_wide, depth, None
    )
    far_order = jnp.concatenate([order[:1], order[3:]])
    queries, keys, values = project(
        far_order, (x_two, x_three), passes, pass_emb, gain_one, shift_one, w_wide, bias_wide, depth, near
    )

    outs, queries = attend(queries, keys, values)

    def slot_of(value, slot):
        return lax.dynamic_index_in_dim(value, order[1 + slot], 0, keepdims=False)

    parts = [slot_of(outs, 0)] + [swap(slot_of(outs, slot), slot) for slot in range(1, passes)]
    pass_row = lax.dynamic_index_in_dim(pass_emb, me, 0, keepdims=True)
    (
        out_rows,
        mixed_grad,
        normed_two,
        activated,
        upper_low,
        proj_low,
        sums,
        up_sum,
        *head_grads,
    ) = middle(
        order[:1],
        parts,
        x_own,
        cotangent[0],
        pass_row,
        full_out,
        full_up,
        full_down,
        out_bias[None],
        ln2_gain[None],
        ln2_bias[None],
        up_bias[None],
        down_bias[None],
    )
    head_grads = [head_grads[0]] + [swap(head_grads[slot], slot) for slot in range(1, passes)]

    by_slot = jnp.stack([dot_tn(part, proj_low) for part in parts]).astype(bfloat)
    out_weight = jnp.concatenate([slot_of(by_slot, slot) for slot in range(passes)], axis=0)
    up_weight = dot_tn(normed_two, upper_low).astype(bfloat)
    down_weight = dot_tn(activated, cotangent[0]).astype(bfloat)
    down_weight = (
        down_weight.reshape(devices, hidden // width, shard, width)
        .transpose(0, 2, 1, 3)
        .reshape(width, hidden)
    )
    reduced = lax.psum_scatter(
        jnp.concatenate([out_weight, up_weight, down_weight], axis=1),
        everyone,
        scatter_dimension=0,
        tiled=True,
    ).astype(single)
    shard_out = reduced[:, :width]
    shard_up = reduced[:, width : width + hidden]
    shard_down = (
        reduced[:, width + hidden :]
        .reshape(shard, hidden // width, width)
        .transpose(1, 0, 2)
        .reshape(w_down.shape)
    )

    qkv_low = attend_back(order[:1], queries, outs, keys, values, head_grads)
    row_parts, head_weight, sums_one, head_bias, pass_sums = project_back(
        order, (x_own, x_one, x_two, x_three), pass_emb, gain_one, shift_one, w_heads, qkv_low
    )

    near_part = swap(row_parts[1], 1)
    far_part = swap(row_parts[3], 1)
    far_sum = (row_parts[2].astype(single) + far_part.astype(single)).astype(bfloat)
    far_sum = swap(far_sum, 2)
    x_grad = (
        mixed_grad
        + row_parts[0].astype(single)
        + near_part.astype(single)
        + far_sum.astype(single)
    )

    scattered = lax.psum_scatter(head_weight, "seq", scatter_dimension=0, tiled=True)
    scattered = scattered.reshape(passes, shard, 3 * group)
    shard_qkv = lax.all_to_all(scattered, "pass", 0, 0, tiled=True)
    shard_qkv = shard_qkv.reshape(passes, shard, 3, group).transpose(1, 2, 0, 3).reshape(w_qkv.shape)

    own_pass = (jnp.arange(passes) == me).astype(single)[:, None]
    pass_part = pass_sums + own_pass * sums[0:1]

    def placed(row):
        return lax.dynamic_update_slice(jnp.zeros((width,), single), row, (me * group,))

    totals = lax.psum(
        jnp.concatenate(
            [
                placed(head_bias[0, :group]),
                placed(head_bias[0, 2 * group :]),
                sums[0],
                sums_one[0],
                sums_one[1],
                sums[1],
                sums[2],
                up_sum[0],
                sums[3],
                pass_part.reshape(-1),
            ]
        ).reshape(-1, width),
        everyone,
    )
    up_rows = hidden // width
    pass_grad = lax.dynamic_slice_in_dim(totals[8 + up_rows :], me, 1, 0)
    return (
        out_rows[None],
        x_grad[None],
        shard_qkv,
        totals[0],
        totals[1],
        shard_out,
        totals[2],
        totals[3],
        totals[4],
        totals[5],
        totals[6],
        shard_up,
        totals[7 : 7 + up_rows].reshape(-1),
        shard_down,
        totals[7 + up_rows],
        pass_grad,
    )


def solution(mesh):
    placed = (
        P("pass", "seq", None),
        P("seq", None),
        P("pass", "seq", None),
        P(),
        P(),
        P(),
        P(("seq", "pass"), None),
        P(),
        P(),
        P(("seq", "pass"), None),
        P(),
        P(),
        P(),
        P(("seq", "pass"), None),
        P(),
        P(("seq", "pass"), None),
        P(),
    )
    return jax.shard_map(
        per_device,
        mesh=mesh,
        in_specs=placed,
        out_specs=(
            P("pass", "seq", None),
            P("pass", "seq", None),
            P(("seq", "pass"), None),
            P(),
            P(),
            P(("seq", "pass"), None),
            P(),
            P(),
            P(),
            P(),
            P(),
            P(("seq", "pass"), None),
            P(),
            P(("seq", "pass"), None),
            P(),
            P("pass", None),
        ),
        check_vma=False,
    )
```

time: 2420 us -> 627 us (0.26)
  waiting for transfers between devices: 1450 us -> 163 us
  local copies, waits for them, and re-layouts: 426 us -> 75.5 us
  matrix products: 328 us -> 22.7 us
  Pallas kernels: 0 us -> 190 us
  loops' own time: 81.3 us -> 0 us
  blocking collectives: 41.1 us -> 104 us
  other arithmetic: 60.7 us -> 21.7 us
    reduce_scatter x6 -> x2, waiting for transfers between devices: 1330 us -> 94.5 us  [the longest x1 94.5 us: per_device(): lax.psum_scatter(jnp.concatenate([out_weight, up_weight, down_weight], ax...]
    dot_general x180 -> x6, matrix products: 328 us -> 22.7 us  [dot_tn(): lax.dot_general(a, b, (((0,), (0,)), ((), ())), preferred_element_type=si...]
    pallas_call x0 -> x6, Pallas kernels: none -> 190 us  [the longest x1 70.9 us: attend_back(): pl.pallas_call(functools.partial(attend_back_kernel, passes, block), grid...]
    all_gather x6 -> x1, waiting for transfers between devices: 111 us -> 0.01 us  [per_device(): lax.all_gather(jnp.concatenate([w_out, w_up, down_cols], axis=1), everyon...]
    another operation x26 -> x0, loops' own time: 81.3 us -> none  [the longest x12 39 us: attend_back(): lax.switch(pass_id, [partial(attend_back_kept, kept) for kept in range(1,...]
    dynamic_update_slice x48 -> x2, local copies, waits for them, and re-layouts: 70.8 us -> 0.43 us  [placed(): lax.dynamic_update_slice(jnp.zeros((width,), single), row, (me * group,))]
    ppermute x0 -> x12, waiting for transfers between devices: none -> 67.2 us  [swap(): lax.ppermute(value, 'pass', [(k, k ^ distance) for k in range(passes)])]
    cond x240 -> x0, local copies, waits for them, and re-layouts: 48 us -> none
  transfers between devices with their start and end apart: 12 -> 17, of which waited for: 9 -> 6; matrix products, arithmetic and copies ran while one was open for 14% -> 13% of each run, Pallas kernels for 0% -> 9%
where the time goes in v1:
time: 627 us; the launch traced here: 617 us
  Pallas kernels  190 us (30%)
  waiting for transfers between devices  163 us (26%)
  blocking collectives  104 us (17%)
  local copies, waits for them, and re-layouts  75.5 us (12%)
  matrix products  22.7 us (4%)
  between operations  22.4 us (4%)
  other arithmetic  21.7 us (3%)
  starting transfers between devices  17.2 us (3%)
    reduce_scatter x1, waiting for transfers between devices, per_device(): lax.psum_scatter(jnp.concatenate([out_weight, up_weight, down_weight], ax...  94.5 us
    pallas_call x1, Pallas kernels, attend_back(): pl.pallas_call(functools.partial(attend_back_kernel, passes, block), grid...  70.9 us
    ppermute x12, waiting for transfers between devices, swap(): lax.ppermute(value, 'pass', [(k, k ^ distance) for k in range(passes)])  67.2 us
    psum x1, blocking collectives, per_device(): lax.psum(jnp.concatenate([placed(head_bias[0, :group]), placed(head_bias[...  67 us
    pallas_call x1, Pallas kernels, attend(): pl.pallas_call(functools.partial(attend_kernel, passes, block), grid=(len...  40.2 us
    pallas_call x1, Pallas kernels, middle(): pl.pallas_call(functools.partial(middle_kernel, groups, 4), grid_spec=plt...  38 us
    all_gather x1, blocking collectives, per_device(): w_heads = lax.all_gather(by_rows, 'seq', axis=0, tiled=True)  37.1 us
    pallas_call x1, Pallas kernels, project_back(): pl.pallas_call(functools.partial(project_back_kernel, count), grid_spec=p...  27.3 us
  transfers between devices with their start and end apart: 17, of which 6 were waited for; matrix products, arithmetic and copies ran while one was open for 13% of the time, Pallas kernels for 9%

profile of v1, /device:TPU:0, one launch (start us, length us, event | category | flops | bytes accessed | tf_op | source)
XLA Modules:
  0.0 616.6 jit_solution(12785624816066151653)
XLA Ops:
  8.3 1.7 pad_maximum_fusion.2
  10.0 3.0 collective-permute-start
  13.0 43.9 %collective-permute-done.refs_0_.refs_2_ = bf16[1024,768]{1,0:T(8,128)(2,1)} collective-permute-done((bf16[1024,768]{1,0:T(8,128)(2,1)}, bf16[1024,768]{1,0:T(8,128)(2,1)}, u32[]{:S(2)}, u32[]{:S(2)}) %collective-permute-start) | collective-permute-done | bytes 1572896 | tf_op jit(solution)/shard_map/ppermute | solution.py:585
  56.9 1.1 reshape.95
  58.9 3.9 all-to-all-start
  71.6 1.7 copy.51.refs_7_
  79.0 37.1 %all_gather.6.refs_7_ = bf16[768,576]{1,0:T(8,128)(2,1)S(1)} all-gather(bf16[96,576]{1,0:T(8,128)(2,1)S(1)} %bitcast.99), channel_id=1, replica_groups=mesh['seq'=8,'pass'=4] {'seq'}, dimensions={0}, use_global_device_ids=true | all-gather | bytes 995328 | tf_op jit(solution)/shard_map/all_gather | solution.py:594
  117.1 1.2 copy-done.7
  118.3 1.4 copy-done.2
  119.7 1.4 copy-done.8
  121.1 6.2 %project.2 = (bf16[3,4,1024,128]{3,2,1,0:T(8,128)(2,1)S(1)}, bf16[3,4,1024,128]{3,2,1,0:T(8,128)(2,1)S(1)}, bf16[3,4,1024,128]{3,2,1,0:T(8,128)(2,1)S(1)}) custom-call(s32[3]{0:T(128)S(1)} %bitcast.88, bf16[1024,768]{1,0:T(8,128)(2,1)S(1)} %bitcast.86, bf16[1024,768]{1,0:T(8,128)(2,1)S(1)} %copy-done.8, f32[4,768]{1,0:T(4,128)S(1)} %copy-done.11, ...), custom_call_target="tpu_custom_call" | custom-call | tf_op jit(solution)/shard_map/project/pallas_call | solution.py:146
  127.4 7.6 %project.3 = (bf16[3,4,1024,128]{3,2,1,0:T(8,128)(2,1)S(1)}, bf16[3,4,1024,128]{3,2,1,0:T(8,128)(2,1)S(1)}, bf16[3,4,1024,128]{3,2,1,0:T(8,128)(2,1)S(1)}) custom-call(s32[3]{0:T(128)S(1)} %pad_add_fusion.me_ref, bf16[1024,768]{1,0:T(8,128)(2,1)} %collective-permute-done.refs_0_.refs_2_, ...), custom_call_target="tpu_custom_call", output_to_operand_aliasing={{0}: (9, {}), {1}: (10, {}), {2}: (11, {})} | custom-call | tf_op jit(solution)/shard_map/project/pallas_call | solution.py:146
  135.0 1.8 copy-done
  136.8 1.6 copy-done.1
  138.4 1.7 copy-done.4
  140.0 40.2 %attend.1 = (bf16[4,1024,192]{2,1,0:T(8,128)(2,1)}, bf16[3,4,1024,128]{3,2,1,0:T(8,128)(2,1)}) custom-call(bf16[3,4,1024,128]{3,2,1,0:T(8,128)(2,1)} %copy-done.4, bf16[3,4,1024,128]{3,2,1,0:T(8,128)(2,1)} %copy-done, bf16[3,4,1024,128]{3,2,1,0:T(8,128)(2,1)} %copy-done.1), custom_call_target="tpu_custom_call" | custom-call | tf_op jit(solution)/shard_map/attend/pallas_call | solution.py:213
  180.2 2.5 dynamic-slice_bitcast_fusion
  182.7 2.4 collective-permute-start.4
  185.3 8.2 %fusion.9 = (bf16[768,3072]{1,0:T(8,128)(2,1)}, bf16[768,3072]{1,0:T(8,128)(2,1)}) fusion(bf16[768,6912]{1,0:T(8,128)(2,1)} %all-gather.2.cloned.1.call-done), kind=kLoop, calls=%fused_computation.63 | loop fusion | bytes 18874368 | tf_op jit(solution)/shard_map/slice | solution.py:603
  193.4 9.7 %reshape.101 = bf16[32,24,4,768]{3,2,1,0:T(4,128)(2,1)} reshape(bf16[768,3072]{1,0:T(8,128)(2,1)} %get-tuple-element.80) | data formatting | bytes 9437184 | tf_op jit(solution)/shard_map/reshape | solution.py:604
  203.2 5.4 copy.53
  208.6 2.4 slice.141.refs_7_
  212.1 38.0 %middle.1 = (bf16[1024,768]{1,0:T(8,128)(2,1)}, f32[1024,768]{1,0:T(8,128)}, bf16[1024,768]{1,0:T(8,128)(2,1)}, bf16[1024,3072]{1,0:T(8,128)(2,1)}, bf16[1024,30...) custom-call(s32[1]{0:T(128)} %bitcast.me_ref, ...), custom_call_target="tpu_custom_call" | custom-call | tf_op jit(solution)/shard_map/middle/pallas_call | solution.py:431
  250.1 2.6 fusion.4
  252.7 10.0 %convolution_convert_fusion = bf16[3072,768]{1,0:T(8,128)(2,1)} fusion(bf16[1024,3072]{1,0:T(8,128)(2,1)} %get-tuple-element.65, bf16[1,1024,768]{2,1,0:T(8,128)(2,1)S(1)} %copy-done.32), kind=kOutput, calls=%fused_computation.1 | convolution fusion | flops 4834197504 | bytes 12582912 | tf_op jit(solution)/shard_map/dot_general | solution.py:32
  262.9 1.9 collective-permute-start.7
  264.8 1.2 fusion.5
  266.0 1.2 fusion.6
  267.3 10.3 %collective-permute-done.7.grad_c = bf16[1024,192]{1,0:T(8,128)(2,1)S(1)} collective-permute-done((bf16[1024,192]{1,0:T(8,128)(2,1)S(1)}, bf16[1024,192]{1,0:T(8,128)(2,1)S(1)}, u32[]{:S(2)}, u32[]{:S(2)}) %collective-permute-start.7) | collective-permute-done | bytes 393248 | tf_op jit(solution)/shard_map/ppermute | solution.py:585
  277.6 10.3 %collective-permute-done.8.grad_d = bf16[1024,192]{1,0:T(8,128)(2,1)S(1)} collective-permute-done((bf16[1024,192]{1,0:T(8,128)(2,1)S(1)}, bf16[1024,192]{1,0:T(8,128)(2,1)S(1)}, u32[]{:S(2)}, u32[]{:S(2)}) %collective-permute-start.8) | collective-permute-done | bytes 393248 | tf_op jit(solution)/shard_map/ppermute | solution.py:585
  288.7 70.9 %attend_back.1.refs_8_ = bf16[4,1024,576]{2,1,0:T(8,128)(2,1)} custom-call(s32[1]{0:T(128)} %bitcast.me_ref, bf16[3,4,1024,128]{3,2,1,0:T(8,128)(2,1)} %get-tuple-element.50.q_ref, bf16[4,1024,192]{2,1,0:T(8,128)(2,1)} %get-tuple-element.47.out_ref, bf16[3,4,1024,128]{3,2,1,0:T(8,128)(2,1)} %copy-done, bf16[3,4,1024,128]{3,2,1,0:T(8,128)(2,1)} %copy-done.1, ...), custom_call_target="tpu_custom_call" | custom-call | tf_op jit(solution)/shard_map/attend_back/pallas_call | solution.py:309
  362.4 27.3 %project_back.1 = (bf16[4,1024,768]{2,1,0:T(8,128)(2,1)}, f32[768,576]{1,0:T(8,128)}, f32[8,768]{1,0:T(8,128)S(1)}, f32[1,576]{1,0:T(1,128)S(1)}, f32[4,768]{1,0:T(4,128)S(1)}) custom-call(s32[5]{0:T(128)S(1)} %copy-done.20, bf16[1024,768]{1,0:T(8,128)(2,1)S(1)} %bitcast.87, bf16[1024,768]{1,0:T(8,128)(2,1)S(1)} %copy-done.9, ...), custom_call_target="tpu_custom_call" | custom-call | tf_op jit(solution)/shard_map/project_back/pallas_call | solution.py:518
  391.6 2.1 fusion.7
  393.7 4.8 copy.55
  398.6 1.0 copy.58
  401.2 5.6 convolution_convert_fusion.1
  406.8 11.2 %pad_maximum_fusion = bf16[768,6912]{1,0:T(8,128)(2,1)} fusion(bf16[768,3072]{1,0:T(8,128)(2,1)S(1)} %bitcast.91, bf16[768,3072]{1,0:T(8,128)(2,1)S(1)} %convolution_convert_fusion.1, bf16[192,768]{1,0:T(8,128)(2,1)S(1)} %get-tuple-element.89, bf16[192,768]{1,0:T(8,128)(2,1)S(1)} %get-tuple-element.90, bf16[192,768]{1,0:T(8,128)(2,1)S(1)} %get-tuple-element.91, ...), kind=kLoop, calls=%fused_computation | loop fusion | flops 63700992 | bytes 21233664 | tf_op jit(solution)/shard_map/concatenate | solution.py:669
  418.1 3.8 slice_bitcast_fusion.1
  423.1 2.6 collective-permute-done.10
  425.7 3.5 fusion
  429.2 1.6 collective-permute-start.11
  431.8 67.0 %psum.7 = f32[16,768]{1,0:T(8,128)S(1)} all-reduce(f32[16,768]{1,0:T(8,128)S(1)} %reshape.107), channel_id=1, replica_groups=mesh['seq'=8,'pass'=4] {'seq','pass'}, use_global_device_ids=true, to_apply=%region_1.2 | all-reduce | flops 12288 | bytes 98304 | tf_op jit(solution)/shard_map/psum | solution.py:710
  499.5 1.2 slice_reduce_fusion
  500.7 3.5 all-to-all-start.1
  504.2 4.9 fusion.3
  511.3 94.5 %reduce-scatter.5.cloned.1.call-done = bf16[24,6912]{1,0:T(8,128)(2,1)} async-done(((bf16[768,6912]{1,0:T(8,128)(2,1)}), bf16[24,6912]{1,0:T(8,128)(2,1)}) %reduce-scatter.5.cloned.1.call-update) | async-done | bytes 331792 | tf_op jit(solution)/shard_map/reduce_scatter | solution.py:668
  605.8 1.7 fusion.10
  608.4 1.4 slice.146
  (177 shorter events, 23.8 us)
Async XLA Ops:
  7.2 66.1 %copy-start.41 = (f32[768]{0:T(1024)S(1)}, f32[768]{0:T(1024)}, u32[]{:S(2)}) copy-start(f32[768]{0:T(1024)} %param.27) | copy-start | bytes 9220
  7.2 66.7 %copy-start.42 = (f32[768]{0:T(1024)S(1)}, f32[768]{0:T(1024)}, u32[]{:S(2)}) copy-start(f32[768]{0:T(1024)} %param.28) | copy-start | bytes 9220
  7.2 67.3 %copy-start.43 = (f32[768]{0:T(1024)S(1)}, f32[768]{0:T(1024)}, u32[]{:S(2)}) copy-start(f32[768]{0:T(1024)} %param.29) | copy-start | bytes 9220
  7.2 67.8 %copy-start.44 = (f32[768]{0:T(1024)S(1)}, f32[768]{0:T(1024)}, u32[]{:S(2)}) copy-start(f32[768]{0:T(1024)} %param.33) | copy-start | bytes 9220
  7.2 71.1 %copy-start.11 = (f32[4,768]{1,0:T(4,128)S(1)}, f32[4,768]{1,0:T(4,128)}, u32[]{:S(2)}) copy-start(f32[4,768]{1,0:T(4,128)} %refs_4_.1) | copy-start | bytes 36868
  7.2 178.0 %all-gather.2.cloned.1.call-start = ((), (), s32[]{:S(2)}) async-start(), calls=%async_computation.4 | async-start | bytes 10948608 | tf_op jit(solution)/shard_map/all_gather | solution.py:597
  10.0 46.9 %collective-permute-start = (bf16[1024,768]{1,0:T(8,128)(2,1)}, bf16[1024,768]{1,0:T(8,128)(2,1)}, u32[]{:S(2)}, u32[]{:S(2)}) collective-permute-start(bf16[1024,768]{1,0:T(8,128)(2,1)} %bitcast.83), channel_id=1, source_target_pairs={{0,2},{1,3},{2,0},{3,1},{4,6},{5,7},{6,4},{7,5},{8,10},{9,11},{10,... | collective-permute-start | bytes 4718600 | tf_op jit(solution)/shard_map/ppermute | solution.py:585
  13.0 103.2 %collective-permute-start.2 = (bf16[1024,768]{1,0:T(8,128)(2,1)}, bf16[1024,768]{1,0:T(8,128)(2,1)S(1)}, u32[]{:S(2)}, u32[]{:S(2)}) collective-permute-start(bf16[1024,768]{1,0:T(8,128)(2,1)} %bitcast.84), channel_id=1, source_target_pairs={{0,1},{1,0},{2,3},{3,2},{4,5},{5,4},{6,7},{7,6},{8,9},{9,8},{10,11... | collective-permute-start | bytes 4718600 | tf_op jit(solution)/shard_map/ppermute | solution.py:585
  56.9 70.5 %collective-permute-start.1 = (bf16[1024,768]{1,0:T(8,128)(2,1)}, bf16[1024,768]{1,0:T(8,128)(2,1)}, u32[]{:S(2)}, u32[]{:S(2)}) collective-permute-start(bf16[1024,768]{1,0:T(8,128)(2,1)} %collective-permute-done.refs_0_.refs_2_), channel_id=1, source_target_pairs={{0,1},{1,0},{2,3},{3,2},{4,5},{5,4},{6,7},{7,6},{8,9},{9,8},{10,11... | collective-permute-start | bytes 4718600 | tf_op jit(solution)/shard_map/ppermute | solution.py:585
  58.9 20.1 %all-to-all-start = ((bf16[4,24,576]{2,1,0:T(8,128)(2,1)}), bf16[4,24,576]{2,1,0:T(8,128)(2,1)S(1)}, u32[]{:S(2)}, u32[]{:S(2)}) async-start(bf16[4,24,576]{2,1,0:T(8,128)(2,1)} %reshape.96), calls=%async_computation | async-start | bytes 245760 | tf_op jit(solution)/shard_map/all_to_all | solution.py:593
  62.7 438.0 %reduce-scatter.3.cloned.1.call-start = ((), (), s32[]{:S(2)}) async-start(), calls=%async_computation.5 | async-start | bytes 2211840 | tf_op jit(solution)/shard_map/reduce_scatter | solution.py:699
  70.9 56.5 %copy-start.13 = (f32[1,768]{1,0:T(1,128)}, f32[1,768]{1,0:T(1,128)S(1)}, u32[]{:S(2)}) copy-start(f32[1,768]{1,0:T(1,128)S(1)} %broadcast_in_dim.38.refs_3_.refs_5_) | copy-start | bytes 9220
  71.6 55.8 %copy-start.15 = (f32[1,768]{1,0:T(1,128)}, f32[1,768]{1,0:T(1,128)S(1)}, u32[]{:S(2)}) copy-start(f32[1,768]{1,0:T(1,128)S(1)} %broadcast_in_dim.39.refs_4_.refs_6_) | copy-start | bytes 9220
  78.3 49.0 %copy-start.19 = (s32[5]{0:T(128)}, s32[5]{0:T(128)S(1)}, u32[]{:S(2)}) copy-start(s32[5]{0:T(128)S(1)} %pad_add_fusion.1.me_ref) | copy-start | bytes 64
  79.0 39.3 %copy-start.10 = (s32[1024,1]{1,0:T(8,128)S(1)}, s32[1024,1]{1,0:T(8,128)}, u32[]{:S(2)}) copy-start(s32[1024,1]{1,0:T(8,128)} %copy.51.refs_7_) | copy-start | bytes 12292
  135.0 1.8 copy-start
  138.4 1.7 copy-start.4
  182.7 28.3 %collective-permute-start.3 = (bf16[1024,192]{1,0:T(8,128)(2,1)S(1)}, bf16[1024,192]{1,0:T(8,128)(2,1)S(1)}, u32[]{:S(2)}, u32[]{:S(2)}) collective-permute-start(bf16[1024,192]{1,0:T(8,128)(2,1)S(1)} %get-tuple-element.86), channel_id=1, source_target_pairs={{0,1},{1,0},{2,3},{3,2},{4,5},{5,4},{6,7},{7,6},{8,9},{9,8},{10,11... | collective-permute-start | bytes 1179656 | tf_op jit(solution)/shard_map/ppermute | solution.py:585
  182.7 28.3 %collective-permute-start.4 = (bf16[1024,192]{1,0:T(8,128)(2,1)S(1)}, bf16[1024,192]{1,0:T(8,128)(2,1)S(1)}, u32[]{:S(2)}, u32[]{:S(2)}) collective-permute-start(bf16[1024,192]{1,0:T(8,128)(2,1)S(1)} %get-tuple-element.85), channel_id=1, source_target_pairs={{0,2},{1,3},{2,0},{3,1},{4,6},{5,7},{6,4},{7,5},{8,10},{9,11},{10,... | collective-permute-start | bytes 1179656 | tf_op jit(solution)/shard_map/ppermute | solution.py:585
  185.1 25.8 %collective-permute-start.5 = (bf16[1024,192]{1,0:T(8,128)(2,1)S(1)}, bf16[1024,192]{1,0:T(8,128)(2,1)S(1)}, u32[]{:S(2)}, u32[]{:S(2)}) collective-permute-start(bf16[1024,192]{1,0:T(8,128)(2,1)S(1)} %get-tuple-element.84), channel_id=1, source_target_pairs={{0,3},{1,2},{2,1},{3,0},{4,7},{5,6},{6,5},{7,4},{8,11},{9,10},{10,... | collective-permute-start | bytes 1179656 | tf_op jit(solution)/shard_map/ppermute | solution.py:585
  212.1 38.0 %copy-start.25 = (bf16[1024,192]{1,0:T(8,128)(2,1)S(1)}, bf16[1024,192]{1,0:T(8,128)(2,1)}, u32[]{:S(2)}) copy-start(bf16[1024,192]{1,0:T(8,128)(2,1)} %get-tuple-element.87.refs_0_) | copy-start | bytes 1179652
  212.1 40.6 %copy-start.32 = (bf16[1,1024,768]{2,1,0:T(8,128)(2,1)S(1)}, bf16[1,1024,768]{2,1,0:T(8,128)(2,1)}, u32[]{:S(2)}) copy-start(bf16[1,1024,768]{2,1,0:T(8,128)(2,1)} %param.19) | copy-start | bytes 4718596
  252.7 10.1 %copy-start.48 = (bf16[1024,192]{1,0:T(8,128)(2,1)S(1)}, bf16[1024,192]{1,0:T(8,128)(2,1)}, u32[]{:S(2)}) copy-start(bf16[1024,192]{1,0:T(8,128)(2,1)} %get-tuple-element.52) | copy-start | bytes 1179652
  252.7 10.1 %copy-start.47 = (bf16[1024,192]{1,0:T(8,128)(2,1)S(1)}, bf16[1024,192]{1,0:T(8,128)(2,1)}, u32[]{:S(2)}) copy-start(bf16[1024,192]{1,0:T(8,128)(2,1)} %get-tuple-element.53) | copy-start | bytes 1179652
  252.7 12.1 %copy-start.46 = (bf16[1024,192]{1,0:T(8,128)(2,1)S(1)}, bf16[1024,192]{1,0:T(8,128)(2,1)}, u32[]{:S(2)}) copy-start(bf16[1024,192]{1,0:T(8,128)(2,1)} %get-tuple-element.54) | copy-start | bytes 1179652
  252.7 12.1 %copy-start.24 = (bf16[1024,768]{1,0:T(8,128)(2,1)S(1)}, bf16[1024,768]{1,0:T(8,128)(2,1)}, u32[]{:S(2)}) copy-start(bf16[1024,768]{1,0:T(8,128)(2,1)} %get-tuple-element.62) | copy-start | bytes 4718596
  252.7 12.1 %copy-start.29 = (bf16[1024,192]{1,0:T(8,128)(2,1)S(1)}, bf16[1024,192]{1,0:T(8,128)(2,1)}, u32[]{:S(2)}) copy-start(bf16[1024,192]{1,0:T(8,128)(2,1)} %copy-done.28) | copy-start | bytes 1179652
  252.7 13.3 %copy-start.31 = (bf16[1024,192]{1,0:T(8,128)(2,1)S(1)}, bf16[1024,192]{1,0:T(8,128)(2,1)}, u32[]{:S(2)}) copy-start(bf16[1024,192]{1,0:T(8,128)(2,1)} %copy-done.30) | copy-start | bytes 1179652
  262.8 4.5 collective-permute-start.6
  262.9 14.7 %collective-permute-start.7 = (bf16[1024,192]{1,0:T(8,128)(2,1)S(1)}, bf16[1024,192]{1,0:T(8,128)(2,1)S(1)}, u32[]{:S(2)}, u32[]{:S(2)}) collective-permute-start(bf16[1024,192]{1,0:T(8,128)(2,1)S(1)} %copy-done.47), channel_id=1, source_target_pairs={{0,2},{1,3},{2,0},{3,1},{4,6},{5,7},{6,4},{7,5},{8,10},{9,11},{10,... | collective-permute-start | bytes 1179656 | tf_op jit(solution)/shard_map/ppermute | solution.py:585
  264.8 23.1 %collective-permute-start.8 = (bf16[1024,192]{1,0:T(8,128)(2,1)S(1)}, bf16[1024,192]{1,0:T(8,128)(2,1)S(1)}, u32[]{:S(2)}, u32[]{:S(2)}) collective-permute-start(bf16[1024,192]{1,0:T(8,128)(2,1)S(1)} %copy-done.46), channel_id=1, source_target_pairs={{0,3},{1,2},{2,1},{3,0},{4,7},{5,6},{6,5},{7,4},{8,11},{9,10},{10,... | collective-permute-start | bytes 1179656 | tf_op jit(solution)/shard_map/ppermute | solution.py:585
  267.3 20.7 %copy-start.36 = (bf16[1024,192]{1,0:T(8,128)(2,1)}, bf16[1024,192]{1,0:T(8,128)(2,1)S(1)}, u32[]{:S(2)}) copy-start(bf16[1024,192]{1,0:T(8,128)(2,1)S(1)} %collective-permute-done.6.grad_b) | copy-start | bytes 1179652
  277.6 10.3 %copy-start.37 = (bf16[1024,192]{1,0:T(8,128)(2,1)}, bf16[1024,192]{1,0:T(8,128)(2,1)S(1)}, u32[]{:S(2)}) copy-start(bf16[1024,192]{1,0:T(8,128)(2,1)S(1)} %collective-permute-done.7.grad_c) | copy-start | bytes 1179652
  288.7 71.0 %copy-start.3 = (bf16[1,1024,768]{2,1,0:T(8,128)(2,1)S(1)}, bf16[1,1024,768]{2,1,0:T(8,128)(2,1)}, u32[]{:S(2)}) copy-start(bf16[1,1024,768]{2,1,0:T(8,128)(2,1)} %param.17) | copy-start | bytes 4718596
  288.7 71.0 %copy-start.6 = (bf16[768,576]{1,0:T(8,128)(2,1)S(1)}, bf16[768,576]{1,0:T(8,128)(2,1)}, u32[]{:S(2)}) copy-start(bf16[768,576]{1,0:T(8,128)(2,1)} %copy-done.5) | copy-start | bytes 2654212
  288.7 71.0 %copy-start.9 = (bf16[1024,768]{1,0:T(8,128)(2,1)S(1)}, bf16[1024,768]{1,0:T(8,128)(2,1)}, u32[]{:S(2)}) copy-start(bf16[1024,768]{1,0:T(8,128)(2,1)} %copy-done.7) | copy-start | bytes 4718596
  391.5 214.2 %reduce-scatter.5.cloned.1.call-start = ((), (), s32[]{:S(2)}) async-start(), calls=%async_computation.6 | async-start | bytes 10948608 | tf_op jit(solution)/shard_map/reduce_scatter | solution.py:668
  393.7 6.2 %slice-start = ((s8[6291456]{0:T(1024)(128)(4,1)}), s8[4194304]{0:T(1024)(128)(4,1)S(1)}, s32[]{:S(2)}) async-start(s8[6291456]{0:T(1024)(128)(4,1)} %bitcast.108), calls=%async_computation.7 | async-start | bytes 8388608
  398.6 1.8 slice-start.1
  418.1 4.2 copy-start.40
  418.1 4.2 copy-start.18
  418.1 4.6 copy-start.22
  422.0 9.8 %copy-start.39 = (f32[1,3072]{1,0:T(1,128)S(1)}, f32[1,3072]{1,0:T(1,128)}, u32[]{:S(2)}) copy-start(f32[1,3072]{1,0:T(1,128)} %get-tuple-element.60) | copy-start | bytes 36868
  422.0 82.2 %copy-start.26 = (f32[1024,768]{1,0:T(8,128)S(1)}, f32[1024,768]{1,0:T(8,128)}, u32[]{:S(2)}) copy-start(f32[1024,768]{1,0:T(8,128)} %get-tuple-element.49) | copy-start | bytes 9437188
  422.0 3.8 collective-permute-start.10
  422.4 81.8 %collective-permute-start.9 = (bf16[1024,768]{1,0:T(8,128)(2,1)}, bf16[1024,768]{1,0:T(8,128)(2,1)}, u32[]{:S(2)}, u32[]{:S(2)}) collective-permute-start(bf16[1024,768]{1,0:T(8,128)(2,1)} %get-tuple-element.82), channel_id=1, source_target_pairs={{0,1},{1,0},{2,3},{3,2},{4,5},{5,4},{6,7},{7,6},{8,9},{9,8},{10,11... | collective-permute-start | bytes 4718600 | tf_op jit(solution)/shard_map/ppermute | solution.py:585
  429.2 75.0 %collective-permute-start.11 = (bf16[1024,768]{1,0:T(8,128)(2,1)}, bf16[1024,768]{1,0:T(8,128)(2,1)}, u32[]{:S(2)}, u32[]{:S(2)}) collective-permute-start(bf16[1024,768]{1,0:T(8,128)(2,1)} %fusion), channel_id=1, source_target_pairs={{0,2},{1,3},{2,0},{3,1},{4,6},{5,7},{6,4},{7,5},{8,10},{9,11},{10,... | collective-permute-start | bytes 4718600 | tf_op jit(solution)/shard_map/ppermute | solution.py:585
  500.7 9.3 %all-to-all-start.1 = ((f32[4,24,576]{2,1,0:T(8,128)}), f32[4,24,576]{2,1,0:T(8,128)S(1)}, u32[]{:S(2)}, u32[]{:S(2)}) async-start(f32[4,24,576]{2,1,0:T(8,128)} %bitcast.101), calls=%async_computation.2 | async-start | bytes 491520 | tf_op jit(solution)/shard_map/all_to_all | solution.py:701
  (20 other events, 19.8 us)
Sparse Core Ops, SparseCore 0:
  11.0 116.6 all-gather.1
  391.7 66.2 reduce-scatter.2
  465.1 140.6 reduce-scatter.4
